TPU v7x, 768 devices: a whole 4x8x12 slice. The times are simulated.
768 devices in a mesh: gx: 16 (over x, y_lo), gy: 48 (over y_hi, z, core).
Axes of the slice: x: 4, y: 8 (y_hi: 2, y_lo: 4; y = y_hi * 4 + y_lo), z: 12, core: 2. Of those that a mesh axis runs over, the one named last changes fastest.
Arguments:
- spin_angles: float32 [2, 2, 4, 1536, 2048], P(None, None, None, 'gy', 'gx'), may hold values from -3.1415927 to 3.1415927, as said below
- species: int32 [2, 4, 1536, 2048], P(None, None, 'gy', 'gx'), may hold values 0 or 1
Outputs:
- spins_next: float32 [2, 3, 4, 1536, 2048], P(None, None, None, 'gy', 'gx')
- dipole_field: float32 [3, 1, 384, 512], P(None, None, 'gy', 'gx')
Inputs may be any that keep to these rules, and one draw needn't show every extreme that they name: `spin_angles`: along dimension 1 the first entry is the polar angle, from 0 to pi, and the second the azimuth. `species`: 0 marks an iron atom and 1 a cobalt atom.
All inputs are finite; a program needn't handle non-finite values. No bound on the sum of `species` on one device may be relied on, other than what follows from the above.
Results may differ from a plain program's by a relative error of at most 0.000075.
Values sent between devices are 32-bit elements; how exact they have to be, the bound alone decides.
A program may use at most 64 MiB of HBM per device.

v0:
```python
import math

import jax
import jax.numpy as jnp
from jax import lax
from jax.sharding import PartitionSpec as P

CELLS_M = 4


DAMPING = 0.1
TIME_STEP = 0.05
EXCHANGE_SCALE = 0.6
DIPOLE = 2.0
MOMENT_PAIR = (2.22, 1.72)
COUPLING_PAIR = (1.0, 1.25)
ANISOTROPY_PAIR = (0.3, 0.9)


def extended(cells, sides, width):
    for axis, dim in sides:
        count = lax.axis_size(axis)
        ends = count - 1
        head = lax.slice_in_dim(cells, 0, width, axis=dim)
        tail = lax.slice_in_dim(cells, cells.shape[dim] - width, cells.shape[dim], axis=dim)
        cells = jnp.concatenate(
            [
                lax.ppermute(tail, axis, [(i, (i + 1) % count) for i in range(ends)]),
                cells,
                lax.ppermute(head, axis, [((i + 1) % count, i) for i in range(ends)]),
            ],
            axis=dim,
        )
    return cells


def species_value(species, table_pair):
    return jnp.where(species == 1, table_pair[1], table_pair[0]).astype(jnp.float32)


def unit_vectors(angles):
    polar_angle = angles[:, 0]
    azimuth = angles[:, 1]
    radial = jnp.sin(polar_angle)
    return jnp.stack(
        [radial * jnp.cos(azimuth), radial * jnp.sin(azimuth), jnp.cos(polar_angle)], axis=1
    )


def box_sum(padded):
    along_x = padded[..., :-1] + padded[..., 1:]
    along_y = along_x[..., :-1, :] + along_x[..., 1:, :]
    return along_y[..., :-1, :, :] + along_y[..., 1:, :, :]


def neighbour_sums(padded):
    corner_side = box_sum(padded[1])[:, :-1, :-1, :-1]
    centre_side = box_sum(padded[0])[:, 1:, 1:, 1:]
    return jnp.stack([corner_side, centre_side])


def cross_product(left_side, right_side):
    return jnp.stack(
        [
            left_side[:, 1] * right_side[:, 2] - left_side[:, 2] * right_side[:, 1],
            left_side[:, 2] * right_side[:, 0] - left_side[:, 0] * right_side[:, 2],
            left_side[:, 0] * right_side[:, 1] - left_side[:, 1] * right_side[:, 0],
        ],
        axis=1,
    )


def torque(vectors, field_total):
    precess = cross_product(vectors, field_total)
    relaxation = cross_product(vectors, precess)
    return -(precess + DAMPING * relaxation) / (1.0 + DAMPING * DAMPING)


def normalized(vectors):
    return vectors / jnp.sqrt(jnp.sum(vectors * vectors, axis=1, keepdims=True))


def total_field(vectors, neighbour_term, exchange_ratio, easy_axis, dipole_atoms):
    along_z = easy_axis * vectors[:, 2]
    zero_part = jnp.zeros_like(along_z)
    field_total = EXCHANGE_SCALE * exchange_ratio[:, None] * neighbour_term + dipole_atoms[None]
    return field_total + jnp.stack([zero_part, zero_part, along_z], axis=1)


def spread_cells(cell_values, repeat):
    dims_in = cell_values.shape
    expanded = jnp.broadcast_to(
        cell_values[:, :, None, :, None, :, None],
        (dims_in[0], dims_in[1], repeat, dims_in[2], repeat, dims_in[3], repeat),
    )
    return expanded.reshape(
        dims_in[0], dims_in[1] * repeat, dims_in[2] * repeat, dims_in[3] * repeat
    )


def wave_numbers(indices, period):
    wrapped = jnp.where(indices < period // 2, indices, indices - period)
    return wrapped.astype(jnp.float32) * (2.0 * math.pi / period)


def forward_table(freqs, places, period):
    product = freqs[:, None] * places[None, :] % period
    phase_angle = product.astype(jnp.float32) * (2.0 * math.pi / period)
    return jnp.stack([jnp.cos(phase_angle), -jnp.sin(phase_angle)])


def apply_kernel(real_part, imag_part, wave_x, wave_y):
    square = wave_x * wave_x + wave_y * wave_y
    length = jnp.sqrt(square)
    inverse = jnp.where(square > 0, 1.0 / jnp.where(square > 0, length, 1.0), 0.0)
    proj_real = wave_x * real_part[0] + wave_y * real_part[1]
    proj_imag = wave_x * imag_part[0] + wave_y * imag_part[1]
    zero_grid = jnp.zeros(proj_real.shape[1:], real_part.dtype)
    x_real = zero_grid
    x_imag = zero_grid
    y_real = zero_grid
    y_imag = zero_grid
    falloff = 0.5 * jnp.exp(-float(abs(0)) * length)
    lateral = inverse * falloff
    x_real = x_real - wave_x * lateral * proj_real[0]
    x_imag = x_imag - wave_x * lateral * proj_imag[0]
    y_real = y_real - wave_y * lateral * proj_real[0]
    y_imag = y_imag - wave_y * lateral * proj_imag[0]
    normal_part = length * falloff - 1.0
    z_real = normal_part * real_part[2, 0]
    z_imag = normal_part * imag_part[2, 0]
    rows_real = [jnp.stack([x_real, y_real, z_real])]
    rows_imag = [jnp.stack([x_imag, y_imag, z_imag])]
    return (jnp.stack(rows_real, axis=1), jnp.stack(rows_imag, axis=1))


def dipole_local(cell_moments):
    cells_y = cell_moments.shape[2]
    cells_x = cell_moments.shape[3]
    groups_y = lax.axis_size("gy")
    groups_x = lax.axis_size("gx")
    size_y = cells_y * groups_y
    size_x = cells_x * groups_x
    period_y = 2 * size_y
    period_x = 2 * size_x
    own_y = 2 * cells_y
    freq_y = lax.axis_index("gy") * own_y + jnp.arange(own_y, dtype=jnp.int32)
    highest = lax.Precision.HIGHEST
    portion = lax.all_gather(cell_moments, "gy", axis=2, tiled=True)
    places = jnp.arange(portion.shape[2], dtype=jnp.int32)
    phases = forward_table(freq_y, places, period_y)
    spectrum = jnp.einsum("rfy,clyx->clrfx", phases, portion, precision=highest)
    own_x = 2 * cells_x
    freq_x = lax.axis_index("gx") * own_x + jnp.arange(own_x, dtype=jnp.int32)
    portion = lax.all_gather(spectrum, "gx", axis=4, tiled=True)
    places = jnp.arange(portion.shape[4], dtype=jnp.int32)
    phases = forward_table(freq_x, places, period_x)
    cos_part = jnp.einsum("clrfx,kx->clrfk", portion, phases[0], precision=highest)
    sin_part = jnp.einsum("clrfx,kx->clrfk", portion, phases[1], precision=highest)
    grid_real = cos_part[:, :, 0] - sin_part[:, :, 1]
    grid_imag = cos_part[:, :, 1] + sin_part[:, :, 0]
    wave_x = wave_numbers(freq_x, period_x)[None, :]
    wave_y = wave_numbers(freq_y, period_y)[:, None]
    field_real, field_imag = apply_kernel(grid_real, grid_imag, wave_x, wave_y)
    places = jnp.arange(cells_x * lax.axis_size("gx"), dtype=jnp.int32)
    phases = forward_table(freq_x, places, period_x)
    out_real = jnp.einsum("kx,clfk->xclf", phases[0], field_real, precision=highest) + jnp.einsum(
        "kx,clfk->xclf", phases[1], field_imag, precision=highest
    )
    out_imag = jnp.einsum("kx,clfk->xclf", phases[0], field_imag, precision=highest) - jnp.einsum(
        "kx,clfk->xclf", phases[1], field_real, precision=highest
    )
    summed = lax.psum_scatter(
        jnp.stack([out_real, out_imag], axis=3), "gx", scatter_dimension=0, tiled=True
    )
    spectrum_mix = jnp.transpose(summed, (1, 2, 3, 4, 0))
    places = jnp.arange(cells_y * lax.axis_size("gy"), dtype=jnp.int32)
    phases = forward_table(freq_y, places, period_y)
    summed_rows = lax.psum_scatter(
        jnp.einsum("fy,clfx->yclx", phases[0], spectrum_mix[:, :, 0], precision=highest)
        + jnp.einsum("fy,clfx->yclx", phases[1], spectrum_mix[:, :, 1], precision=highest),
        "gy",
        scatter_dimension=0,
        tiled=True,
    )
    return DIPOLE / (period_x * period_y) * jnp.transpose(summed_rows, (1, 2, 0, 3))


def on_device(spin_angles, species):
    vectors = unit_vectors(spin_angles)
    moment = species_value(species, MOMENT_PAIR)
    coupling = species_value(species, COUPLING_PAIR)
    exchange_ratio = coupling / moment
    easy_axis = 2.0 * species_value(species, ANISOTROPY_PAIR) / moment
    layers = species.shape[1] // CELLS_M
    cells_y = species.shape[2] // CELLS_M
    cells_x = species.shape[3] // CELLS_M
    scaled = (moment[:, None] * vectors).reshape(
        2, 3, layers, CELLS_M, cells_y, CELLS_M, cells_x, CELLS_M
    )
    cell_moments = jnp.sum(scaled, axis=(0, 3, 5, 7)) / (2 * CELLS_M * CELLS_M * CELLS_M)
    dipole_field = dipole_local(cell_moments)
    dipole_atoms = spread_cells(dipole_field, CELLS_M)

    def neighbours(spin_vecs):
        weighted = coupling[:, None] * spin_vecs
        widened = extended(weighted, (("gx", 4), ("gy", 3)), 1)
        padded = jnp.pad(widened, ((0, 0), (0, 0), (1, 1), (0, 0), (0, 0)))
        return neighbour_sums(padded)

    field_first = total_field(vectors, neighbours(vectors), exchange_ratio, easy_axis, dipole_atoms)
    torque_first = torque(vectors, field_first)
    predicted = normalized(vectors + TIME_STEP * torque_first)
    field_second = total_field(
        predicted, neighbours(predicted), exchange_ratio, easy_axis, dipole_atoms
    )
    torque_second = torque(predicted, field_second)
    spins_next = normalized(vectors + 0.5 * TIME_STEP * (torque_first + torque_second))
    return (spins_next, dipole_field)


def solution(mesh):
    in_specs = (P(None, None, None, "gy", "gx"), P(None, None, "gy", "gx"))
    out_specs = (P(None, None, None, "gy", "gx"), P(None, None, "gy", "gx"))
    return jax.shard_map(
        on_device, mesh=mesh, in_specs=in_specs, out_specs=out_specs, check_vma=False
    )
```

profile of v0, /device:TPU:1, one launch (start us, length us, event | category | flops | bytes accessed | tf_op | source)
XLA Modules:
  0.0 841.4 jit_solution(8537530144152485522)
XLA Ops:
  7.2 1.8 fusion.25
  9.1 2.1 fusion.30
  13.0 4.0 collective-permute-start
  18.3 5.7 stack.100
  24.0 5.7 stack.101
  29.7 5.7 stack.102
  35.4 3.3 copy.61
  38.7 3.3 copy.62
  42.0 5.7 mul.681
  47.7 3.3 copy.60
  51.0 3.3 copy.63
  54.5 87.8 %all-gather = f32[3,384,32]{2,1,0:T(8,128)S(1)} all-gather(f32[3,8,32]{2,1,0:T(8,128)S(1)} %broadcast_multiply_fusion.2), channel_id=2, replica_groups=mesh['gx'=16,'gy'=48] {'gy'}, dimensions={1}, use_global_device_ids=true | all-gather | bytes 150528 | tf_op jit(solution)/shard_map/all_gather | solution.py:149
  143.1 53.7 %all_gather.7 = f32[3,1,2,16,512]{3,2,1,0,4:T(2,128)S(1)} all-gather(f32[3,1,2,16,32]{3,2,1,0,4:T(2,128)S(1)} %copy.64), channel_id=1, replica_groups=mesh['gx'=16,'gy'=48] {'gx'}, dimensions={4}, use_global_device_ids=true | all-gather | bytes 208896 | tf_op jit(solution)/shard_map/all_gather | solution.py:155
  204.7 1.9 collective-permute-start.2
  206.6 7.6 collective-permute-start.3
  215.0 1.9 copy.81
  223.2 71.9 %reduce-scatter.4.cloned.1.call-done = f32[32,96]{1,0:T(8,128)} async-done(((f32[512,96]{1,0:T(8,128)}), f32[32,96]{1,0:T(8,128)}) %reduce-scatter.4.cloned.1.call-update) | async-done | bytes 12304
  298.8 497.9 %all-reduce.7.cloned.1.call-done = f32[384,3,1,32]{3,2,1,0:T(1,128)} async-done(((f32[384,3,1,32]{3,2,1,0:T(1,128)}), f32[384,3,1,32]{3,2,1,0:T(1,128)}) %all-reduce.7.cloned.1.call-update) | async-done | bytes 147472
  801.2 2.2 collective-permute-start.4
  804.7 6.2 collective-permute-done.4
  810.9 13.3 %collective-permute-done.5 = f32[2,3,4,32,1]{4,3,2,1,0:T(8,128)S(1)} collective-permute-done((f32[2,3,4,32,1]{4,3,2,1,0:T(8,128)S(1)}, f32[2,3,4,32,1]{4,3,2,1,0:T(8,128)S(1)}, u32[]{:S(2)}, u32[]{:S(2)}) %collective-permute-start.5) | collective-permute-done | bytes 3104 | tf_op jit(solution)/shard_map/ppermute | solution.py:30
  824.4 1.9 collective-permute-start.6
  826.3 2.4 collective-permute-start.7
  828.8 2.7 collective-permute-done.7
  (96 shorter events, 30.8 us)
Async XLA Ops:
  7.2 287.9 %reduce-scatter.4.cloned.1.call-start = ((), (), s32[]{:S(2)}) async-start(), calls=%async_computation.1 | async-start | bytes 278528
  11.2 1.8 copy-start.5
  11.9 12.2 %copy-start.2 = (f32[2,4,32,128]{3,2,1,0:T(8,128)}, f32[2,4,32,128]{3,2,1,0:T(8,128)S(1)}, u32[]{:S(2)}) copy-start(f32[2,4,32,128]{3,2,1,0:T(8,128)S(1)} %get-tuple-element.53) | copy-start | bytes 393220
  13.0 190.0 %collective-permute-start = (f32[2,3,4,32,1]{4,3,2,0,1:T(8,128)}, f32[2,3,4,32,1]{4,3,2,0,1:T(8,128)S(1)}, u32[]{:S(2)}, u32[]{:S(2)}) collective-permute-start(f32[2,3,4,32,1]{4,3,2,0,1:T(8,128)} %get-tuple-element.44), channel_id=1, source_target_pairs={{0,48},{48,96},{96,144},{144,192},{192,240},{240,288},{288,336},{3... | collective-permute-start | bytes 9224 | tf_op jit(solution)/shard_map/ppermute | solution.py:28
  17.0 185.9 %collective-permute-start.1 = (f32[2,3,4,32,1]{4,3,2,0,1:T(8,128)}, f32[2,3,4,32,1]{4,3,2,0,1:T(8,128)}, u32[]{:S(2)}, u32[]{:S(2)}) collective-permute-start(f32[2,3,4,32,1]{4,3,2,0,1:T(8,128)} %get-tuple-element.45), channel_id=1, source_target_pairs={{48,0},{96,48},{144,96},{192,144},{240,192},{288,240},{336,288},{3... | collective-permute-start | bytes 9224 | tf_op jit(solution)/shard_map/ppermute | solution.py:30
  204.7 16.0 %collective-permute-start.2 = (f32[2,3,4,1,130]{4,3,2,0,1:T(1,128)}, f32[2,3,4,1,130]{4,3,2,0,1:T(1,128)}, u32[]{:S(2)}, u32[]{:S(2)}) collective-permute-start(f32[2,3,4,1,130]{4,3,2,0,1:T(1,128)} %get-tuple-element.32), channel_id=1, source_target_pairs={{0,1},{1,2},{2,3},{3,4},{4,5},{5,6},{6,7},{7,8},{8,9},{9,10},{10,1... | collective-permute-start | bytes 37448 | tf_op jit(solution)/shard_map/ppermute | solution.py:28
  206.6 14.0 %collective-permute-start.3 = (f32[2,3,4,1,130]{4,3,2,0,1:T(1,128)}, f32[2,3,4,1,130]{4,3,2,0,1:T(1,128)}, u32[]{:S(2)}, u32[]{:S(2)}) collective-permute-start(f32[2,3,4,1,130]{4,3,2,0,1:T(1,128)} %get-tuple-element.33), channel_id=1, source_target_pairs={{1,0},{2,1},{3,2},{4,3},{5,4},{6,5},{7,6},{8,7},{9,8},{10,9},{11,1... | collective-permute-start | bytes 37448 | tf_op jit(solution)/shard_map/ppermute | solution.py:30
  218.7 578.0 %all-reduce.7.cloned.1.call-start = ((), (), s32[]{:S(2)}) async-start(), calls=%async_computation.2 | async-start | bytes 1179648
  798.0 1.4 copy-start.1
  798.0 1.4 copy-start.4
  798.2 1.2 copy-start
  799.9 0.9 copy-start.3
  801.0 27.8 %copy-start.6 = (pred[2,4,32,128]{3,2,1,0:T(8,128)(4,1)S(1)}, pred[2,4,32,128]{3,2,1,0:T(8,128)(4,1)}, u32[]{:S(2)}) copy-start(pred[2,4,32,128]{3,2,1,0:T(8,128)(4,1)} %copy-done.5) | copy-start | bytes 98308
  801.2 9.7 %collective-permute-start.4 = (f32[2,3,4,32,1]{4,3,2,1,0:T(8,128)S(1)}, f32[2,3,4,32,1]{4,3,2,1,0:T(8,128)S(1)}, u32[]{:S(2)}, u32[]{:S(2)}) collective-permute-start(f32[2,3,4,32,1]{4,3,2,1,0:T(8,128)S(1)} %get-tuple-element.42), channel_id=1, source_target_pairs={{0,48},{48,96},{96,144},{144,192},{192,240},{240,288},{288,336},{3... | collective-permute-start | bytes 9224 | tf_op jit(solution)/shard_map/ppermute | solution.py:28
  803.4 20.8 %collective-permute-start.5 = (f32[2,3,4,32,1]{4,3,2,1,0:T(8,128)S(1)}, f32[2,3,4,32,1]{4,3,2,1,0:T(8,128)S(1)}, u32[]{:S(2)}, u32[]{:S(2)}) collective-permute-start(f32[2,3,4,32,1]{4,3,2,1,0:T(8,128)S(1)} %get-tuple-element.43), channel_id=1, source_target_pairs={{48,0},{96,48},{144,96},{192,144},{240,192},{288,240},{336,288},{3... | collective-permute-start | bytes 9224 | tf_op jit(solution)/shard_map/ppermute | solution.py:30
  824.4 4.4 collective-permute-start.6
  826.3 5.1 collective-permute-start.7
Sparse Core Ops, SparseCore 0:
  218.8 76.2 reduce-scatter.3
  298.7 497.9 all-reduce.6
where the time goes:
time: 845 us; the launch traced here: 841 us
  waiting for transfers between devices  592 us (70%)
  blocking collectives  141 us (17%)
  local copies, waits for them, and re-layouts  48.7 us (6%)
  starting transfers between devices  22.8 us (3%)
  between operations  15.3 us (2%)
  other arithmetic  14.9 us (2%)
    unnamed x4, waiting for transfers between devices  570 us
    all_gather x1, blocking collectives, dipole_local(): portion = lax.all_gather(cell_moments, 'gy', axis=2, tiled=True)  87.8 us
    all_gather x1, blocking collectives, dipole_local(): portion = lax.all_gather(spectrum, 'gx', axis=4, tiled=True)  53.7 us
    another operation x6, local copies, waits for them, and re-layouts, unit_vectors(): jnp.stack([radial * jnp.cos(azimuth), radial * jnp.sin(azimuth), jnp.cos(...  26.9 us
  transfers between devices with their start and end apart: 10, of which 5 were waited for; matrix products, arithmetic and copies ran while one was open for 6% of the time, Pallas kernels for 0%

commit v1 on v0

v1 whole, which is shorter than its diff:
```python
import functools
import math

import jax
import jax.numpy as jnp
import numpy as np
from jax import lax
from jax.experimental import pallas as pl
from jax.experimental.pallas import tpu as pltpu
from jax.sharding import PartitionSpec as P

MESH = pl.DeviceIdType.MESH
HIGHEST = lax.Precision.HIGHEST
F32 = jnp.float32

CELLS_M = 4
DAMPING = 0.1
TIME_STEP = 0.05
EXCHANGE_SCALE = 0.6
DIPOLE = 2.0
MOMENT_PAIR = (2.22, 1.72)
COUPLING_PAIR = (1.0, 1.25)
ANISOTROPY_PAIR = (0.3, 0.9)
RATIO_PAIR = (COUPLING_PAIR[0] / MOMENT_PAIR[0], COUPLING_PAIR[1] / MOMENT_PAIR[1])
EASY_PAIR = (2 * ANISOTROPY_PAIR[0] / MOMENT_PAIR[0], 2 * ANISOTROPY_PAIR[1] / MOMENT_PAIR[1])

PART_K = 32
ROWS = 8
COLS = 32
WINDOWS = 10
TABLE_LEAD = 8
TABLE_ROWS = 400


def wave_tables(nx, ny):
    period_x, period_y = 2 * nx * COLS, 2 * ny * ROWS
    half_y = period_y // 2
    v = np.arange(period_x // 2 + 1)
    u = np.arange(half_y + 1)
    a = 2 * np.pi * v[:, None] / period_x
    b = 2 * np.pi * u[None, :] / period_y
    k = np.sqrt(a * a + b * b)
    inv = np.where(k > 0, 1.0 / np.where(k > 0, k, 1.0), 0.0)
    g = {
        "xx": -a * a * 0.5 * inv,
        "yy": -b * b * 0.5 * inv,
        "zz": 0.5 * k - 1.0,
        "xy": -a * b * 0.5 * inv,
    }
    dy = np.arange(-TABLE_LEAD, TABLE_ROWS - TABLE_LEAD)
    angle = 2 * np.pi * ((u[:, None] * dy[None, :]) % period_y) / period_y
    fold = np.where((u == 0) | (u == half_y), 1.0, 2.0)
    cosine = fold[:, None] * np.cos(angle)
    sine = np.where((u == 0) | (u == half_y), 0.0, 2.0)[:, None] * np.sin(angle)
    scale = DIPOLE / (period_x * period_y) * np.where((v == 0) | (v == period_x // 2), 1.0, 2.0)
    tables = [scale[:, None] * (g[n] @ cosine) for n in ("xx", "yy", "zz")]
    odd = scale[:, None] * (g["xy"] @ sine)
    odd[-1] = 0.0
    tables.append(odd)
    lanes = np.stack(tables)
    out = np.zeros((nx + 1, TABLE_ROWS, 4 * PART_K), np.float32)
    for s in range(nx):
        block = lanes[:, s * PART_K : (s + 1) * PART_K, :]
        out[s] = block.transpose(2, 0, 1).reshape(TABLE_ROWS, -1)
    out[nx] = out[0]
    for n in range(4):
        out[nx, :, n * PART_K] = lanes[n, -1, :]
    corner = DIPOLE / (period_x * period_y) * float(-0.5 * np.pi * np.pi / np.sqrt(2 * np.pi**2))
    return out, corner


def trig_tables(nx):
    period = 2 * nx * COLS
    lane = np.arange(128)
    comp = np.where(lane < 96, lane // 32, np.where(lane < 102, (lane - 96) // 2, 3))
    place = np.where(lane < 96, lane % 32, np.where(lane % 2 == 0, -1, 32))
    j = np.arange(PART_K)
    t = 2 * np.pi * ((j[:, None] * place[None, :]) % period) / period
    base = np.stack([np.cos(t), np.sin(t)]).astype(np.float32)
    s = np.arange(nx)
    t = 2 * np.pi * ((s[:, None] * PART_K * place[None, :]) % period) / period
    phase = np.stack([np.cos(t), np.sin(t)], axis=1).astype(np.float32)
    jl = lane % 32
    t = 2 * np.pi * ((s[:, None] * COLS * jl[None, :]) % period) / period
    twist = np.stack([np.cos(t), np.sin(t)]).astype(np.float32)
    row = np.stack([comp, np.where(place % 2 == 0, 1, -1)]).astype(np.float32)
    return base, phase, twist, row


def sine(r):
    q = r * r
    p = 1.0 / 6227020800.0
    for c in (-1.0 / 39916800.0, 1.0 / 362880.0, -1.0 / 5040.0, 1.0 / 120.0, -1.0 / 6.0):
        p = p * q + c
    return r + r * q * p


def sine_cosine(x):
    size = jnp.abs(x)
    far = (np.float32(math.pi) - size) + np.float32(math.pi - float(np.float32(math.pi)))
    s = sine(jnp.where(size > np.float32(math.pi / 2), far, size))
    half = (np.float32(math.pi / 2) - size) + np.float32(
        math.pi / 2 - float(np.float32(math.pi / 2))
    )
    return jnp.where(x < 0, -s, s), sine(half)


def pick(cobalt, pair):
    return jnp.where(cobalt, np.float32(pair[1]), np.float32(pair[0]))


def unit(polar, azimuth):
    sp, cp = sine_cosine(polar)
    sq, cq = sine_cosine(azimuth)
    return sp * cq, sp * sq, cp


def iota(shape, dim):
    return lax.broadcasted_iota(jnp.int32, shape, dim)


def gather_kernel(
    nx, ny, corner,
    ang, spc, table_hbm, base, phase, twist, lanes,
    fld, hy_ang, hy_spc, hx, hc,
    mom, tile, b_a, q_mat, tab, tab2, up, dn, b_b, send_c, b_c, pack, g_ang, g_spc, g_x, g_c,
    tab_sem, s_a, r_a, s_b, r_b, s_c, r_c, s_h, r_h,
):
    gx, gy = lax.axis_index("gx"), lax.axis_index("gy")
    left, right = lax.rem(gx + nx - 1, nx), lax.rem(gx + 1, nx)
    below, above = lax.rem(gy + ny - 1, ny), lax.rem(gy + 1, ny)

    loads = [
        pltpu.make_async_copy(table_hbm.at[gx], tab.at[0], tab_sem.at[0]),
        pltpu.make_async_copy(table_hbm.at[jnp.where(gx == 0, nx, gx)], tab.at[1], tab_sem.at[1]),
    ]
    for load in loads:
        load.start()

    barrier = pltpu.get_barrier_semaphore()

    def hail(device):
        pl.semaphore_signal(barrier, inc=1, device_id=device, device_id_type=MESH)

    @pl.loop(1, ny)
    def _(o):
        hail((gx, lax.rem(gy + o, ny)))

    @pl.loop(1, nx)
    def _(o):
        hail((lax.rem(gx + o, nx), gy))

    for device in ((left, below), (right, below), (left, above), (right, above)):
        hail(device)

    def remote(src, dst, send, recv, device):
        return pltpu.make_async_remote_copy(
            src_ref=src, dst_ref=dst, send_sem=send, recv_sem=recv, device_id=device, device_id_type=MESH
        )

    total = [jnp.zeros((32, 128), F32) for _ in range(3)]
    for sub in range(2):
        for z in range(4):
            moment = pick(spc[sub, z] == 1, MOMENT_PAIR)
            v = unit(ang[sub, 0, z], ang[sub, 1, z])
            total = [t + moment * c for t, c in zip(total, v)]
    x_cell, l_cell = iota((128, 128), 0) >> 2, iota((128, 128), 1)
    packed = jnp.zeros((8, 128), F32)
    for c in range(3):
        mom[c] = total[c]
        rows = mom[c, pl.ds(0, 8, 4), :]
        for r in range(1, 4):
            rows = rows + mom[c, pl.ds(r, 8, 4), :]
        spread = jnp.where(l_cell == x_cell + 32 * c, np.float32(1 / 128), np.float32(0))
        packed = packed + jnp.dot(rows, spread, precision=HIGHEST, preferred_element_type=F32)
    tile[...] = packed

    lane = iota((128, 128), 1)
    edges = jnp.zeros((128, 128), F32)
    for q in range(3):
        for sub in range(2):
            n = 2 * q + sub
            block = ang[sub, q] if q < 2 else spc[sub].astype(F32)
            block = block.reshape(128, 128)
            edges = jnp.where(lane == n, pltpu.roll(block, n, 1) if n else block, edges)
            edges = jnp.where(lane == 8 + n, pltpu.roll(block, n + 9, 1), edges)
    edges = jnp.transpose(edges)
    pack[0] = edges[0:8]
    pack[1] = edges[8:16]

    b_cos, b_sin = base[0], base[1]
    p_cos, p_sin = phase[gx, 0:1, :], phase[gx, 1:2, :]
    cosine = b_cos * p_cos - b_sin * p_sin
    sinus = b_sin * p_cos + b_cos * p_sin
    comp, parity = lanes[0:1, :], lanes[1:2, :]
    single = (iota((32, 128), 0) + gx) == 0
    for c in range(3):
        mine = comp == np.float32(c)
        real, imag = (sinus, cosine) if c == 1 else (cosine, -sinus)
        q_mat[pl.ds(32 * c, 32), :] = jnp.where(mine, jnp.where(single, 1.0, real), 0.0)
        q_mat[pl.ds(128 + 32 * c, 32), :] = jnp.where(mine, jnp.where(single, parity, imag), 0.0)
    q_mat[pl.ds(96, 32), :] = jnp.zeros((32, 128), F32)
    q_mat[pl.ds(224, 32), :] = jnp.zeros((32, 128), F32)

    for load in loads:
        load.wait()
    wide = iota((TABLE_ROWS, 128), 1)
    for p in range(2):
        t = tab[p]
        tab2[p] = jnp.where(
            wide < 32,
            pltpu.roll(t, 32, 1),
            jnp.where(wide < 64, -pltpu.roll(t, 64, 1), 0.0),
        )

    pl.semaphore_wait(barrier, nx - 1 + ny - 1 + 4)

    @pl.loop(1, nx)
    def _(o):
        to = lax.rem(gx + o, nx)
        remote(tile, b_a.at[gx], s_a.at[o], r_a.at[gx], (to, gy)).start()

    halos = [
        remote(ang.at[:, :, :, pl.ds(31, 1), :], g_ang.at[:, :, :, pl.ds(0, 1), :], s_h.at[0], r_h.at[0], (gx, above)),
        remote(ang.at[:, :, :, pl.ds(0, 1), :], g_ang.at[:, :, :, pl.ds(1, 1), :], s_h.at[1], r_h.at[1], (gx, below)),
        remote(spc.at[:, :, pl.ds(31, 1), :], g_spc.at[:, :, pl.ds(0, 1), :], s_h.at[2], r_h.at[2], (gx, above)),
        remote(spc.at[:, :, pl.ds(0, 1), :], g_spc.at[:, :, pl.ds(1, 1), :], s_h.at[3], r_h.at[3], (gx, below)),
        remote(pack.at[1], g_x.at[0], s_h.at[4], r_h.at[4], (right, gy)),
        remote(pack.at[0], g_x.at[1], s_h.at[5], r_h.at[5], (left, gy)),
        remote(pack.at[1], g_c.at[0], s_h.at[6], r_h.at[6], (right, above)),
        remote(pack.at[0], g_c.at[1], s_h.at[7], r_h.at[7], (left, above)),
        remote(pack.at[1], g_c.at[2], s_h.at[8], r_h.at[8], (right, below)),
        remote(pack.at[0], g_c.at[3], s_h.at[9], r_h.at[9], (left, below)),
    ]
    for copy in halos:
        copy.start()

    b_a[gx] = packed

    @pl.loop(1, nx)
    def _(o):
        src = lax.rem(gx + o, nx)
        remote(tile, b_a.at[src], s_a.at[0], r_a.at[src], (gx, gy)).wait_recv()

    wave = lax.dot_general(
        b_a[...].reshape(nx * 8, 128), q_mat[...], (((1,), (1,)), ((), ())),
        precision=HIGHEST, preferred_element_type=F32,
    )
    real = jnp.zeros((8, 128), F32)
    imag = jnp.zeros((8, 128), F32)
    for g in range(nx):
        t_re, t_im = wave[8 * g : 8 * g + 8, 0:128], wave[8 * g : 8 * g + 8, 128:256]
        c, s = twist[0, g : g + 1, :], twist[1, g : g + 1, :]
        real = real + (t_re * c + t_im * s)
        imag = imag + (t_im * c - t_re * s)

    lane8 = iota((8, 128), 1)
    is_y = (lane8 >= 32) & (lane8 < 64)
    flip = jnp.where(is_y, np.float32(-1), np.float32(1))
    dn[0] = real * flip
    dn[1] = imag * flip
    for r in range(8):
        up[0, r : r + 1, :] = real[7 - r : 8 - r]
        up[1, r : r + 1, :] = imag[7 - r : 8 - r]

    @pl.loop(1, ny)
    def _(o):
        to = gy + o

        @pl.when(to < ny)
        def _():
            remote(up, b_b.at[gy], s_b.at[o], r_b.at[gy], (gx, to)).start()

        @pl.when(to >= ny)
        def _():
            remote(dn, b_b.at[gy], s_b.at[o], r_b.at[gy], (gx, to - ny)).start()

    zero = jnp.zeros((8, 128), F32)

    def swapped(s):
        return jnp.where(lane8 < 32, pltpu.roll(s, 96, 1), pltpu.roll(s, 32, 1))

    def add_source(d, parts, acc):
        acc = list(acc)
        for p in range(2):
            s = parts[p]
            t = swapped(s)
            for w in range(WINDOWS):
                rows = pl.ds(8 * d + w, 8)
                acc[2 * w + p] = acc[2 * w + p] + tab[p, rows, :] * s + tab2[p, rows, :] * t
        acc[-1] = acc[-1] + parts[1]
        return tuple(acc)

    def arrive(src):
        remote(up, b_b.at[src], s_b.at[0], r_b.at[src], (gx, gy)).wait_recv()
        return b_b[src, 0], b_b[src, 1]

    start = tuple(zero for _ in range(2 * WINDOWS + 1))
    acc_up = add_source(0, (up[0], up[1]), start)
    acc_up = lax.fori_loop(1, gy + 1, lambda d, a: add_source(d, arrive(gy - d), a), acc_up)
    acc_dn = lax.fori_loop(1, ny - gy, lambda d, a: add_source(d, arrive(gy + d), a), start)

    alternate = jnp.where(iota((8, 128), 0) % 2 == 0, np.float32(1), np.float32(-1))
    last = jnp.sum((flip * acc_dn[-1] - acc_up[-1]) * alternate, axis=0, keepdims=True)
    last = jnp.broadcast_to(last, (8, 128))
    last = swapped(last)
    last = jnp.where(((lane8 == 0) | (lane8 == 32)) & (gx == 0), last, 0.0) * np.float32(corner)

    row16 = iota((16, 128), 0)
    field = []
    for p in range(2):
        out = jnp.zeros((16, 128), F32)
        for w in range(WINDOWS):
            sums = acc_up[2 * w + p] + flip * acc_dn[2 * (WINDOWS - 1 - w) + p]
            if p == 1:
                sign = np.float32((1 if w % 2 else -1) / 8)
                sums = sums + sign * last
            line = jnp.sum(sums, axis=0, keepdims=True)
            out = jnp.where(row16 == w, jnp.broadcast_to(line, (16, 128)), out)
        field.append(out)

    turned = []
    for g in range(nx):
        c, s = twist[0, g : g + 1, :], twist[1, g : g + 1, :]
        turned.append(
            jnp.concatenate([field[0] * c - field[1] * s, field[0] * s + field[1] * c], axis=1)
        )
    turned = jnp.concatenate(turned, axis=0)
    shares = jnp.dot(turned, q_mat[...], precision=HIGHEST, preferred_element_type=F32)
    send_c[...] = shares.reshape(nx, 16, 128)

    @pl.loop(1, nx)
    def _(o):
        to = lax.rem(gx + o, nx)
        remote(send_c.at[to], b_c.at[gx], s_c.at[o], r_c.at[gx], (to, gy)).start()

    b_c[gx] = send_c[gx]
    for copy in halos:
        copy.wait_recv()
    hy_ang[...] = g_ang[...]
    hy_spc[...] = g_spc[...]
    hx[...] = g_x[...]
    hc[...] = g_c[...]

    @pl.loop(1, nx)
    def _(o):
        src = lax.rem(gx + o, nx)
        remote(send_c.at[0], b_c.at[src], s_c.at[0], r_c.at[src], (gx, gy)).wait_recv()

    whole = b_c[0]
    for g in range(1, nx):
        whole = whole + b_c[g]
    fld[...] = whole

    for copy in halos:
        copy.wait_send()

    @pl.loop(1, nx)
    def _(o):
        remote(tile, b_a.at[0], s_a.at[o], r_a.at[0], (gx, gy)).wait_send()
        remote(send_c.at[0], b_c.at[0], s_c.at[o], r_c.at[0], (gx, gy)).wait_send()

    @pl.loop(1, ny)
    def _(o):
        remote(up, b_b.at[0], s_b.at[o], r_b.at[0], (gx, gy)).wait_send()


def cross(a, b):
    return (
        a[1] * b[2] - a[2] * b[1],
        a[2] * b[0] - a[0] * b[2],
        a[0] * b[1] - a[1] * b[0],
    )


def torque(v, h):
    p = cross(v, h)
    r = cross(v, p)
    return [
        (a + np.float32(DAMPING) * b) * np.float32(-1.0 / (1.0 + DAMPING * DAMPING))
        for a, b in zip(p, r)
    ]


def normalized(w):
    s = w[0] * w[0] + w[1] * w[1] + w[2] * w[2]
    r = lax.rsqrt(s)
    r = r * (1.5 - 0.5 * s * r * r)
    return [c * r for c in w]


def heun_kernel(
    nx, ny,
    ang, spc, fld, hy_ang, hy_spc, hx, hc, lanes,
    nxt, dip,
    raw, cpl, vec, wgt, dpl,
):
    gx, gy = lax.axis_index("gx"), lax.axis_index("gy")
    for c in range(3):
        dip[c, 0] = fld[1:9, 32 * c : 32 * c + 32]

    comp = iota((128, 256), 0)
    atom = iota((128, 256), 1)
    want = jnp.where(atom < 128, atom >> 2, jnp.where(atom < 192, 97, 96))
    scale = jnp.where(atom < 128, 32, 2)
    row8 = iota((8, 256), 0)
    for c in range(3):
        hot = jnp.where(comp == want + scale * c, np.float32(1), np.float32(0))
        lines = jnp.dot(fld[...], hot, precision=HIGHEST, preferred_element_type=F32)

        def line(w):
            return jnp.broadcast_to(lines[w : w + 1], (8, 256))

        for t in range(4):
            dpl[c, pl.ds(8 * t, 8), :] = jnp.where(row8 < 4, line(2 * t + 1), line(2 * t + 2))
        dpl[c, pl.ds(32, 8), :] = jnp.where(row8 < 4, line(9), line(0))

    cols = jnp.concatenate(
        [hx[0], hx[1], hc[0], hc[1], hc[2], hc[3], jnp.zeros((80, 128), F32)], axis=0
    )
    cols = jnp.transpose(cols)
    lane32 = iota((32, 128), 1)
    lane8, rowh = iota((8, 128), 1), iota((8, 128), 0)

    for q in range(3):
        for sub in range(2):
            n = 2 * q + sub
            for z in range(4):

                def column(piece):
                    part = cols[32 * z : 32 * z + 32, 8 * piece + n : 8 * piece + n + 1]
                    return jnp.broadcast_to(part, (32, 128))

                def spot(piece, y):
                    part = cols[32 * z + y : 32 * z + y + 1, 8 * piece + n : 8 * piece + n + 1]
                    return jnp.broadcast_to(part, (8, 128))

                def edge(side):
                    if q < 2:
                        return jnp.broadcast_to(hy_ang[sub, q, z, side : side + 1, :], (8, 128))
                    return jnp.broadcast_to(hy_spc[sub, z, side : side + 1, :], (8, 128)).astype(F32)

                raw[n, z, 0:32, 0:128] = ang[sub, q, z] if q < 2 else spc[sub, z].astype(F32)
                raw[n, z, 0:32, 128:256] = jnp.where(lane32 < 64, column(1), column(0))
                raw[n, z, 32:40, 0:128] = jnp.where(rowh < 4, edge(1), edge(0))
                low = jnp.where(lane8 < 64, spot(3, 31), spot(2, 31))
                high = jnp.where(lane8 < 64, spot(5, 0), spot(4, 0))
                raw[n, z, 32:40, 128:256] = jnp.where(rowh < 4, high, low)

    row = iota((40, 256), 0)
    col = iota((40, 256), 1)
    y = gy * 32 + jnp.where(row < 36, row, row - 40)
    x = gx * 128 + jnp.where(col < 192, col, col - 256)
    inside = (y >= 0) & (y < ny * 32) & (x >= 0) & (x < nx * 128)

    for sub in range(2):
        for z in range(4):
            cobalt = raw[4 + sub, z] > 0.5
            coupling = jnp.where(inside, pick(cobalt, COUPLING_PAIR), 0.0)
            cpl[sub, z] = coupling
            v = unit(raw[sub, z], raw[2 + sub, z])
            for c in range(3):
                vec[sub, c, z] = v[c]
                wgt[sub, c, z] = coupling * v[c]

    def neighbours(sub, c, z):
        other = 1 - sub
        near = wgt[other, c, z]
        far = z - 1 if sub == 0 else z + 1
        if 0 <= far < 4:
            near = near + wgt[other, c, far]
        near = near + pltpu.roll(near, 1 if sub == 0 else 255, 1)
        return near + pltpu.roll(near, 1 if sub == 0 else 39, 0)

    def total_field(sub, z, v, n, cobalt, d):
        ratio = pick(cobalt, [np.float32(EXCHANGE_SCALE) * np.float32(r) for r in RATIO_PAIR])
        h = [ratio * n[c] + d[c] for c in range(3)]
        h[2] = h[2] + pick(cobalt, EASY_PAIR) * v[2]
        return h

    ahead = {}
    for sub in range(2):
        for z in range(4):
            cobalt = raw[4 + sub, z] > 0.5
            v = [vec[sub, c, z] for c in range(3)]
            n = [neighbours(sub, c, z) for c in range(3)]
            f = torque(v, total_field(sub, z, v, n, cobalt, [dpl[c] for c in range(3)]))
            p = normalized([a + np.float32(TIME_STEP) * b for a, b in zip(v, f)])
            for c in range(3):
                raw[3 * sub + c, z] = p[c]
                nxt[sub, c, z] = f[c][0:32, 0:128]
    for sub in range(2):
        for z in range(4):
            for c in range(3):
                wgt[sub, c, z] = cpl[sub, z] * raw[3 * sub + c, z]
    for sub in range(2):
        for z in range(4):
            cobalt = spc[sub, z] == 1
            p = [raw[3 * sub + c, z, 0:32, 0:128] for c in range(3)]
            n = [neighbours(sub, c, z)[0:32, 0:128] for c in range(3)]
            d = [dpl[c, 0:32, 0:128] for c in range(3)]
            f = torque(p, total_field(sub, z, p, n, cobalt, d))
            w = [
                vec[sub, c, z, 0:32, 0:128] + np.float32(0.5 * TIME_STEP) * (nxt[sub, c, z] + f[c])
                for c in range(3)
            ]
            w = normalized(w)
            for c in range(3):
                nxt[sub, c, z] = w[c]


def solution(mesh):
    nx, ny = mesh.shape["gx"], mesh.shape["gy"]
    table, corner = wave_tables(nx, ny)
    base, phase, twist, lanes = trig_tables(nx)
    vmem = pl.BlockSpec(memory_space=pltpu.VMEM)
    dma = pltpu.SemaphoreType.DMA

    def scratch(*shape, dtype=F32):
        return pltpu.VMEM(shape, dtype)

    def on_device(spin_angles, species):
        halves = pl.pallas_call(
            functools.partial(gather_kernel, nx, ny, corner),
            out_shape=[
                jax.ShapeDtypeStruct((16, 128), F32),
                jax.ShapeDtypeStruct((2, 2, 4, 2, 128), F32),
                jax.ShapeDtypeStruct((2, 4, 2, 128), jnp.int32),
                jax.ShapeDtypeStruct((2, 8, 128), F32),
                jax.ShapeDtypeStruct((4, 8, 128), F32),
            ],
            in_specs=[vmem, vmem, pl.BlockSpec(memory_space=pl.ANY), vmem, vmem, vmem, vmem],
            out_specs=[vmem] * 5,
            scratch_shapes=[
                scratch(3, 32, 128),
                scratch(8, 128),
                scratch(nx, 8, 128),
                scratch(256, 128),
                scratch(2, TABLE_ROWS, 128),
                scratch(2, TABLE_ROWS, 128),
                scratch(2, 8, 128),
                scratch(2, 8, 128),
                scratch(ny, 2, 8, 128),
                scratch(nx, 16, 128),
                scratch(nx, 16, 128),
                scratch(2, 8, 128),
                scratch(2, 2, 4, 2, 128),
                scratch(2, 4, 2, 128, dtype=jnp.int32),
                scratch(2, 8, 128),
                scratch(4, 8, 128),
                dma((2,)),
                dma((nx,)),
                dma((nx,)),
                dma((ny,)),
                dma((ny,)),
                dma((nx,)),
                dma((nx,)),
                dma((10,)),
                dma((10,)),
            ],
            compiler_params=pltpu.CompilerParams(collective_id=0, has_side_effects=True),
        )(spin_angles, species, table, base, phase, twist, lanes)
        fld, hy_ang, hy_spc, hx, hc = halves
        return pl.pallas_call(
            functools.partial(heun_kernel, nx, ny),
            out_shape=[
                jax.ShapeDtypeStruct((2, 3, 4, 32, 128), F32),
                jax.ShapeDtypeStruct((3, 1, 8, 32), F32),
            ],
            in_specs=[vmem] * 8,
            out_specs=[vmem] * 2,
            scratch_shapes=[
                scratch(6, 4, 40, 256),
                scratch(2, 4, 40, 256),
                scratch(2, 3, 4, 40, 256),
                scratch(2, 3, 4, 40, 256),
                scratch(3, 40, 256),
            ],
        )(spin_angles, species, fld, hy_ang, hy_spc, hx, hc, lanes)

    return jax.shard_map(
        lambda a, s: tuple(on_device(a, s)),
        mesh=mesh,
        in_specs=(P(None, None, None, "gy", "gx"), P(None, None, "gy", "gx")),
        out_specs=(P(None, None, None, "gy", "gx"), P(None, None, "gy", "gx")),
        check_vma=False,
    )
```

time: 845 us -> 60.7 us (0.07)
  waiting for transfers between devices: 592 us -> 0 us
  blocking collectives: 141 us -> 0 us
  Pallas kernels: 0 us -> 59.9 us
  local copies, waits for them, and re-layouts: 48.7 us -> 0 us
  starting transfers between devices: 22.8 us -> 0 us
  other arithmetic: 14.9 us -> 0 us
  between operations: 15.3 us -> 0.64 us
    unnamed x4 -> x0, waiting for transfers between devices: 570 us -> none
    all_gather x2 -> x0, blocking collectives: 141 us -> none  [the longest x1 87.8 us: dipole_local(): portion = lax.all_gather(cell_moments, 'gy', axis=2, tiled=True)]
    pallas_call x0 -> x2, Pallas kernels: none -> 59.9 us  [the longest x1 55.4 us: on_device(): pl.pallas_call(functools.partial(gather_kernel, nx, ny, corner), out_shap...]
    another operation x6 -> x0, local copies, waits for them, and re-layouts: 26.9 us -> none  [unit_vectors(): jnp.stack([radial * jnp.cos(azimuth), radial * jnp.sin(azimuth), jnp.cos(...]
    ppermute x8 -> x0, starting transfers between devices: 22.7 us -> none  [the longest x4 12.6 us: extended(): lax.ppermute(head, axis, [((i + 1) % count, i) for i in range(ends)])]
    ppermute x8 -> x0, waiting for transfers between devices: 22.1 us -> none  [the longest x4 15.9 us: extended(): lax.ppermute(head, axis, [((i + 1) % count, i) for i in range(ends)])]
    mul x2 -> x0, local copies, waits for them, and re-layouts: 9 us -> none  [on_device(): moment[:, None] * vectors]
  transfers between devices with their start and end apart: 10 -> 0, of which waited for: 5 -> 0; matrix products, arithmetic and copies ran while one was open for 6% -> 0% of each run, Pallas kernels for 0% -> 0%
where the time goes in v1:
time: 60.7 us; the launch traced here: 60.5 us
  Pallas kernels  59.9 us (99%)
  between operations  0.64 us (1%)
    pallas_call x1, Pallas kernels, on_device(): pl.pallas_call(functools.partial(gather_kernel, nx, ny, corner), out_shap...  55.4 us
    pallas_call x1, Pallas kernels, on_device(): pl.pallas_call(functools.partial(heun_kernel, nx, ny), out_shape=[jax.Sha...  4.5 us

profile of v1, /device:TPU:1, one launch (start us, length us, event | category | flops | bytes accessed | tf_op | source)
XLA Modules:
  0.0 60.5 jit_solution(1467964026043220559)
XLA Ops:
  0.6 55.4 %shard_map.86 = (f32[16,128]{1,0:T(8,128)}, f32[2,2,4,2,128]{4,3,2,1,0:T(2,128)}, s32[2,4,2,128]{3,2,1,0:T(2,128)}, f32[2,8,128]{2,1,0:T(8,128)}, f32[4,8,128]{2,1,0:T(8,128)}) custom-call(f32[2,2,4,32,128]{4,3,2,1,0:T(8,128)} %ang.3, s32[2,4,32,128]{3,2,1,0:T(8,128)} %spc.3, f32[17,400,128]{2,1,0:T(8,128)} %constant.10.clone.table_hbm, ...), custom_call_target="tpu_custom_call" | custom-call | tf_op jit(solution)/shard_map/pallas_call | solution.py:523
  56.0 4.5 %shard_map.87 = (f32[2,3,4,32,128]{4,3,2,1,0:T(8,128)}, f32[3,1,8,32]{3,2,1,0:T(8,128)}) custom-call(f32[2,2,4,32,128]{4,3,2,1,0:T(8,128)} %ang.3, s32[2,4,32,128]{3,2,1,0:T(8,128)} %spc.3, f32[16,128]{1,0:T(8,128)} %get-tuple-element.7.fld, f32[2,2,4,2,128]{4,3,2,1,0:T(2,128)} %get-tuple-element.8.hy_ang, s32[2,4,2,128]{3,2,1,0:T(2,128)} %get-tuple-element.9.hy_spc, ...), custom_call_target="tpu_custom_call" | custom-call | tf_op jit(solution)/shard_map/pallas_call | solution.py:564

commit v2 on v1

v2 whole, which is shorter than its diff:
```python
import functools
import math

import jax
import jax.numpy as jnp
import numpy as np
from jax import lax
from jax.experimental import pallas as pl
from jax.experimental.pallas import tpu as pltpu
from jax.sharding import PartitionSpec as P

MESH = pl.DeviceIdType.MESH
F32, BF16 = jnp.float32, jnp.bfloat16

CELLS_M = 4
DAMPING = 0.1
TIME_STEP = 0.05
EXCHANGE_SCALE = 0.6
DIPOLE = 2.0
MOMENT_PAIR = (2.22, 1.72)
COUPLING_PAIR = (1.0, 1.25)
ANISOTROPY_PAIR = (0.3, 0.9)
RATIO_PAIR = (COUPLING_PAIR[0] / MOMENT_PAIR[0], COUPLING_PAIR[1] / MOMENT_PAIR[1])
EASY_PAIR = (2 * ANISOTROPY_PAIR[0] / MOMENT_PAIR[0], 2 * ANISOTROPY_PAIR[1] / MOMENT_PAIR[1])

PART_K = 32
ROWS = 8
COLS = 32
WINDOWS = 10
TABLE_LEAD = 8
TABLE_ROWS = 400


def wave_tables(nx, ny):
    period_x, period_y = 2 * nx * COLS, 2 * ny * ROWS
    half_y = period_y // 2
    v = np.arange(period_x // 2 + 1)
    u = np.arange(half_y + 1)
    a = 2 * np.pi * v[:, None] / period_x
    b = 2 * np.pi * u[None, :] / period_y
    k = np.sqrt(a * a + b * b)
    inv = np.where(k > 0, 1.0 / np.where(k > 0, k, 1.0), 0.0)
    g = {
        "xx": -a * a * 0.5 * inv,
        "yy": -b * b * 0.5 * inv,
        "zz": 0.5 * k - 1.0,
        "xy": -a * b * 0.5 * inv,
    }
    dy = np.arange(-TABLE_LEAD, TABLE_ROWS - TABLE_LEAD)
    angle = 2 * np.pi * ((u[:, None] * dy[None, :]) % period_y) / period_y
    fold = np.where((u == 0) | (u == half_y), 1.0, 2.0)
    cosine = fold[:, None] * np.cos(angle)
    sine = np.where((u == 0) | (u == half_y), 0.0, 2.0)[:, None] * np.sin(angle)
    scale = DIPOLE / (period_x * period_y) * np.where((v == 0) | (v == period_x // 2), 1.0, 2.0)
    tables = [scale[:, None] * (g[n] @ cosine) for n in ("xx", "yy", "zz")]
    odd = scale[:, None] * (g["xy"] @ sine)
    odd[-1] = 0.0
    tables.append(odd)
    lanes = np.stack(tables)
    out = np.zeros((nx + 1, TABLE_ROWS, 4 * PART_K), np.float32)
    for s in range(nx):
        block = lanes[:, s * PART_K : (s + 1) * PART_K, :]
        out[s] = block.transpose(2, 0, 1).reshape(TABLE_ROWS, -1)
    out[nx] = out[0]
    for n in range(4):
        out[nx, :, n * PART_K] = lanes[n, -1, :]
    corner = DIPOLE / (period_x * period_y) * float(-0.5 * np.pi * np.pi / np.sqrt(2 * np.pi**2))
    return out, corner


def trig_tables(nx):
    period = 2 * nx * COLS
    lane = np.arange(128)
    comp = np.where(lane < 96, lane // 32, np.where(lane < 102, (lane - 96) // 2, 3))
    place = np.where(lane < 96, lane % 32, np.where(lane % 2 == 0, -1, 32))
    j = np.arange(PART_K)
    t = 2 * np.pi * ((j[:, None] * place[None, :]) % period) / period
    base = np.stack([np.cos(t), np.sin(t)]).astype(np.float32)
    s = np.arange(nx)
    t = 2 * np.pi * ((s[:, None] * PART_K * place[None, :]) % period) / period
    phase = np.stack([np.cos(t), np.sin(t)], axis=1).astype(np.float32)
    jl = lane % 32
    t = 2 * np.pi * ((s[:, None] * COLS * jl[None, :]) % period) / period
    twist = np.stack([np.cos(t), np.sin(t)]).astype(np.float32)
    row = np.stack([comp, np.where(place % 2 == 0, 1, -1)]).astype(np.float32)
    return base, phase, twist, row


def sine(r):
    q = r * r
    p = 1.0 / 6227020800.0
    for c in (-1.0 / 39916800.0, 1.0 / 362880.0, -1.0 / 5040.0, 1.0 / 120.0, -1.0 / 6.0):
        p = p * q + c
    return r + r * q * p


def sine_cosine(x):
    size = jnp.abs(x)
    far = (np.float32(math.pi) - size) + np.float32(math.pi - float(np.float32(math.pi)))
    s = sine(jnp.where(size > np.float32(math.pi / 2), far, size))
    half = (np.float32(math.pi / 2) - size) + np.float32(
        math.pi / 2 - float(np.float32(math.pi / 2))
    )
    return jnp.where(x < 0, -s, s), sine(half)


def pick(cobalt, pair):
    return jnp.where(cobalt, np.float32(pair[1]), np.float32(pair[0]))


def unit(polar, azimuth):
    sp, cp = sine_cosine(polar)
    sq, cq = sine_cosine(azimuth)
    return sp * cq, sp * sq, cp


def iota(shape, dim):
    return lax.broadcasted_iota(jnp.int32, shape, dim)


def cross(a, b):
    return (
        a[1] * b[2] - a[2] * b[1],
        a[2] * b[0] - a[0] * b[2],
        a[0] * b[1] - a[1] * b[0],
    )


def torque(v, h):
    p = cross(v, h)
    r = cross(v, p)
    return [
        (a + np.float32(DAMPING) * b) * np.float32(-1.0 / (1.0 + DAMPING * DAMPING))
        for a, b in zip(p, r)
    ]


def normalized(w):
    s = w[0] * w[0] + w[1] * w[1] + w[2] * w[2]
    r = lax.rsqrt(s)
    r = r * (1.5 - 0.5 * s * r * r)
    return [c * r for c in w]


def split(x, pieces):
    out = []
    for _ in range(pieces):
        out.append(x.astype(BF16))
        x = x - out[-1].astype(F32)
    return out


def dot(a, b, dims=(1, 0)):
    return lax.dot_general(
        a, b, (((dims[0],), (dims[1],)), ((), ())), preferred_element_type=F32
    )


def exact_dot(a, hot):
    n = a.shape[0]
    out = dot(jnp.concatenate(split(a, 3), axis=0), hot)
    return out[0:n] + out[n : 2 * n] + out[2 * n : 3 * n]


def wide_dot(a, b_high, b_low, dims):
    n = a.shape[0]
    high, low = split(a, 2)
    out = dot(jnp.concatenate([high, low], axis=0), b_high, dims)
    return out[0:n] + out[n : 2 * n] + dot(high, b_low, dims)


def step_kernel(
    nx, ny, corner,
    ang_hbm, spc_hbm, table_hbm, base, phase, twist, lanes,
    nxt, dip,
    ang, spc, mom, tile, b_a, q_high, q_low, tab, tab2, up, dn, b_b, send_c, b_c, pack, g_ang, g_spc, g_x, g_c,
    raw, cpl, vec, wgt, fix, dpl,
    load_sem, s_a, r_a, s_b, r_b, s_f, r_f, s_c, r_c, s_h, r_h, rise, fall,
):
    gx, gy = lax.axis_index("gx"), lax.axis_index("gy")
    left, right = lax.rem(gx + nx - 1, nx), lax.rem(gx + 1, nx)
    below, above = lax.rem(gy + ny - 1, ny), lax.rem(gy + 1, ny)
    core = lax.rem(gy, 2)
    chip = gy // 2
    partner = gy + 1 - 2 * core
    chips = ny // 2
    half = ny // 2
    row = lax.rem(gy, half)
    z_up = gy - row + lax.rem(row + 2, half)
    z_down = gy - row + lax.rem(row + half - 2, half)
    opposite = lax.rem(gy + half, ny)

    loads = []
    for sub in range(2):
        loads.append(pltpu.make_async_copy(ang_hbm.at[sub], ang.at[sub], load_sem.at[2 * sub]))
        loads.append(pltpu.make_async_copy(spc_hbm.at[sub], spc.at[sub], load_sem.at[2 * sub + 1]))
    late_loads = [
        pltpu.make_async_copy(table_hbm.at[gx], tab.at[0], load_sem.at[4]),
        pltpu.make_async_copy(table_hbm.at[jnp.where(gx == 0, nx, gx)], tab.at[1], load_sem.at[5]),
    ]
    for load in loads + late_loads:
        load.start()

    barrier = pltpu.get_barrier_semaphore()

    def signal(semaphore, device):
        pl.semaphore_signal(semaphore, inc=1, device_id=device, device_id_type=MESH)

    @pl.loop(1, nx)
    def _(o):
        signal(barrier, (lax.rem(gx + o, nx), gy))

    for other in (above, below, z_up, z_down, opposite):
        signal(barrier, (gx, other))

    def remote(src, dst, send, recv, device):
        return pltpu.make_async_remote_copy(
            src_ref=src, dst_ref=dst, send_sem=send, recv_sem=recv, device_id=device, device_id_type=MESH
        )

    total = [jnp.zeros((32, 128), F32) for _ in range(3)]
    for sub in range(2):
        loads[2 * sub].wait()
        loads[2 * sub + 1].wait()
        for z in range(4):
            moment = pick(spc[sub, z] == 1, MOMENT_PAIR)
            v = unit(ang[sub, 0, z], ang[sub, 1, z])
            for c in range(3):
                vec[sub, c, z, 0:32, 0:128] = v[c]
            total = [t + moment * c for t, c in zip(total, v)]
    rows = []
    for c in range(3):
        mom[c] = total[c]
        line = mom[c, pl.ds(0, 8, 4), :]
        for r in range(1, 4):
            line = line + mom[c, pl.ds(r, 8, 4), :]
        rows.append(line)
    atom = iota((384, 128), 0)
    place = ((atom >> 7) << 5) + ((atom & 127) >> 2)
    spread = jnp.where(iota((384, 128), 1) == place, 1 / 128, 0.0).astype(BF16)
    packed = exact_dot(jnp.concatenate(rows, axis=1), spread)
    tile[...] = packed

    pl.semaphore_wait(barrier, nx - 1 + 5)

    @pl.loop(1, nx)
    def _(o):
        remote(tile, b_a.at[gx], s_a, r_a, (lax.rem(gx + o, nx), gy)).start()

    def tell(t):
        signal(rise.at[t], (gx, z_up))
        signal(fall.at[t], (gx, z_down))

    def hear(t):
        pl.semaphore_wait(rise.at[t], 1)
        pl.semaphore_wait(fall.at[t], 1)

    hops = half // 4
    halo_row, halo_spc, halo_x, halo_c = [
        [remote(src, dst, s_h.at[n], r_h.at[n], to) for src, dst, to in pair]
        for n, pair in enumerate((
            ((ang.at[:, :, :, pl.ds(31, 1), :], g_ang.at[:, :, :, pl.ds(0, 1), :], (gx, above)),
             (ang.at[:, :, :, pl.ds(0, 1), :], g_ang.at[:, :, :, pl.ds(1, 1), :], (gx, below))),
            ((spc.at[:, :, pl.ds(31, 1), :], g_spc.at[:, :, pl.ds(0, 1), :], (gx, above)),
             (spc.at[:, :, pl.ds(0, 1), :], g_spc.at[:, :, pl.ds(1, 1), :], (gx, below))),
            ((pack.at[1], g_x.at[0], (right, gy)), (pack.at[0], g_x.at[1], (left, gy))),
            ((g_x, g_c.at[0], (gx, above)), (g_x, g_c.at[1], (gx, below))),
        ))
    ]
    halo_all = [remote(g, g, s_h.at[n], r_h.at[n], (gx, gy)) for n, g in enumerate((g_ang, g_spc, g_x, g_c))]

    tell(0)
    b_a[gx] = packed

    lane = iota((128, 128), 1)
    edges = jnp.zeros((128, 128), F32)
    for q in range(3):
        for sub in range(2):
            n = 2 * q + sub
            block = ang[sub, q] if q < 2 else spc[sub].astype(F32)
            block = block.reshape(128, 128)
            edges = jnp.where(lane == n, pltpu.roll(block, n, 1) if n else block, edges)
            edges = jnp.where(lane == 8 + n, pltpu.roll(block, n + 9, 1), edges)
    edges = jnp.transpose(edges)
    pack[0] = edges[0:8]
    pack[1] = edges[8:16]
    for copy in halo_x + halo_row + halo_spc:
        copy.start()
    hear(0)
    tell(1)

    b_cos, b_sin = base[0], base[1]
    p_cos, p_sin = phase[gx, 0:1, :], phase[gx, 1:2, :]
    cosine = b_cos * p_cos - b_sin * p_sin
    sinus = b_sin * p_cos + b_cos * p_sin
    comp, parity = lanes[0:1, :], lanes[1:2, :]
    single = (iota((32, 128), 0) + gx) == 0

    def store_q(at, q):
        q_high[pl.ds(at, 32), :], q_low[pl.ds(at, 32), :] = split(q, 2)

    for c in range(3):
        mine = comp == np.float32(c)
        real, imag = (sinus, cosine) if c == 1 else (cosine, -sinus)
        store_q(32 * c, jnp.where(mine, jnp.where(single, 1.0, real), 0.0))
        store_q(128 + 32 * c, jnp.where(mine, jnp.where(single, parity, imag), 0.0))
    store_q(96, jnp.zeros((32, 128), F32))
    store_q(224, jnp.zeros((32, 128), F32))
    hear(1)
    tell(2)

    for load in late_loads:
        load.wait()
    wide = iota((TABLE_ROWS, 128), 1)
    for p in range(2):
        t = tab[p]
        tab2[p] = jnp.where(
            wide < 32,
            pltpu.roll(t, 32, 1),
            jnp.where(wide < 64, -pltpu.roll(t, 64, 1), 0.0),
        )
        hear(2 + p)
        tell(3 + p)
    for t in range(4, hops):
        hear(t)
        if t + 1 < hops:
            tell(t + 1)

    def blocks(ref, n, send, recv):
        return remote(ref.at[pl.ds(0, n)], ref.at[pl.ds(0, n)], send, recv, (gx, gy))

    blocks(b_a, nx - 1, s_a, r_a).wait_recv()

    wave = wide_dot(b_a[...].reshape(nx * 8, 128), q_high[...], q_low[...], (1, 1))
    real = jnp.zeros((8, 128), F32)
    imag = jnp.zeros((8, 128), F32)
    for g in range(nx):
        t_re, t_im = wave[8 * g : 8 * g + 8, 0:128], wave[8 * g : 8 * g + 8, 128:256]
        c, s = twist[0, g : g + 1, :], twist[1, g : g + 1, :]
        real = real + (t_re * c + t_im * s)
        imag = imag + (t_im * c - t_re * s)

    lane8 = iota((8, 128), 1)
    is_y = (lane8 >= 32) & (lane8 < 64)
    flip = jnp.where(is_y, np.float32(-1), np.float32(1))
    dn[0] = real * flip
    dn[1] = imag * flip
    for r in range(8):
        up[0, r : r + 1, :] = real[7 - r : 8 - r]
        up[1, r : r + 1, :] = imag[7 - r : 8 - r]

    @pl.loop(1, chips)
    def _(k):
        to = lax.rem(gy + 2 * k, ny)

        @pl.when(to > gy)
        def _():
            remote(up, b_b.at[core, chip], s_b, r_b, (gx, to)).start()

        @pl.when(to < gy)
        def _():
            remote(dn, b_b.at[core, chip], s_b, r_b, (gx, to)).start()

    even = core == 0
    b_b[core, chip] = jnp.where(even, up[...], dn[...])

    halo_all[2].wait_recv()
    for copy in halo_c:
        copy.start()
    halo_all[0].wait_recv()
    halo_all[1].wait_recv()
    halo_all[3].wait_recv()

    cols = jnp.concatenate(
        [g_x[0], g_x[1], g_c[0, 0], g_c[0, 1], g_c[1, 0], g_c[1, 1], jnp.zeros((80, 128), F32)], axis=0
    )
    cols = jnp.transpose(cols)
    lane32 = iota((32, 128), 1)
    rowh = iota((8, 128), 0)
    for q in range(3):
        for sub in range(2):
            n = 2 * q + sub
            for z in range(4):

                def column(piece):
                    part = cols[32 * z : 32 * z + 32, 8 * piece + n : 8 * piece + n + 1]
                    return jnp.broadcast_to(part, (32, 128))

                def spot(piece, y):
                    part = cols[32 * z + y : 32 * z + y + 1, 8 * piece + n : 8 * piece + n + 1]
                    return jnp.broadcast_to(part, (8, 128))

                def edge(side):
                    if q < 2:
                        return jnp.broadcast_to(g_ang[sub, q, z, side : side + 1, :], (8, 128))
                    return jnp.broadcast_to(g_spc[sub, z, side : side + 1, :], (8, 128)).astype(F32)

                if q == 2:
                    raw[n, z, 0:32, 0:128] = spc[sub, z].astype(F32)
                raw[n, z, 0:32, 128:256] = jnp.where(lane32 < 64, column(1), column(0))
                raw[n, z, 32:40, 0:128] = jnp.where(rowh < 4, edge(1), edge(0))
                low = jnp.where(lane8 < 64, spot(3, 31), spot(2, 31))
                high = jnp.where(lane8 < 64, spot(5, 0), spot(4, 0))
                raw[n, z, 32:40, 128:256] = jnp.where(rowh < 4, high, low)

    at_row = iota((40, 256), 0)
    at_col = iota((40, 256), 1)
    y = gy * 32 + jnp.where(at_row < 36, at_row, at_row - 40)
    x = gx * 128 + jnp.where(at_col < 192, at_col, at_col - 256)
    inside = (y >= 0) & (y < ny * 32) & (x >= 0) & (x < nx * 128)
    for sub in range(2):
        for z in range(4):
            for r, l in ((slice(0, 32), slice(128, 256)), (slice(32, 40), slice(0, 256))):
                v = unit(raw[sub, z, r, l], raw[2 + sub, z, r, l])
                for c in range(3):
                    vec[sub, c, z, r, l] = v[c]
            coupling = jnp.where(inside, pick(raw[4 + sub, z] > 0.5, COUPLING_PAIR), 0.0)
            cpl[sub, z] = coupling
            for c in range(3):
                wgt[sub, c, z] = coupling * vec[sub, c, z]

    def neighbours(sub, c, z):
        other = 1 - sub
        near = wgt[other, c, z]
        far = z - 1 if sub == 0 else z + 1
        if 0 <= far < 4:
            near = near + wgt[other, c, far]
        near = near + pltpu.roll(near, 1 if sub == 0 else 255, 1)
        return near + pltpu.roll(near, 1 if sub == 0 else 39, 0)

    ratio_pair = [np.float32(EXCHANGE_SCALE) * np.float32(r) for r in RATIO_PAIR]
    for sub in range(2):
        for z in range(4):
            cobalt = raw[4 + sub, z] > 0.5
            ratio = pick(cobalt, ratio_pair)
            for c in range(3):
                h = ratio * neighbours(sub, c, z)
                if c == 2:
                    h = h + pick(cobalt, EASY_PAIR) * vec[sub, c, z]
                fix[sub, c, z] = h

    blocks(b_b.at[core], chips - 1, s_b, r_b).wait_recv()
    hand_on = remote(b_b.at[core], b_b.at[core], s_f, r_f, (gx, partner))
    hand_on.start()

    zero = jnp.zeros((8, 128), F32)

    def swapped(s):
        return jnp.where(lane8 < 32, pltpu.roll(s, 96, 1), pltpu.roll(s, 32, 1))

    def add_source(d, parts, acc):
        acc = list(acc)
        for p in range(2):
            s = parts[p]
            t = swapped(s)
            for w in range(WINDOWS):
                span = pl.ds(8 * d + w, 8)
                acc[2 * w + p] = acc[2 * w + p] + tab[p, span, :] * s + tab2[p, span, :] * t
        acc[-1] = acc[-1] + parts[1]
        return tuple(acc)

    def add_chips(which, acc_up, acc_dn):
        def source(k):
            return b_b[which, k, 0], b_b[which, k, 1]

        acc_up = lax.fori_loop(
            0, chip, lambda k, a: add_source(gy - (2 * k + which), source(k), a), acc_up
        )
        acc_dn = lax.fori_loop(
            chip + 1, chips, lambda k, a: add_source(2 * k + which - gy, source(k), a), acc_dn
        )
        return acc_up, acc_dn

    start = tuple(zero for _ in range(2 * WINDOWS + 1))
    acc_up = add_source(0, (up[0], up[1]), start)
    acc_up, acc_dn = add_chips(core, acc_up, start)
    blocks(b_b.at[1 - core], chips, s_f, r_f).wait_recv()
    acc_up, acc_dn = add_chips(1 - core, acc_up, acc_dn)
    beside = (b_b[1 - core, chip, 0], b_b[1 - core, chip, 1])
    acc_up = lax.fori_loop(0, core, lambda _, a: add_source(1, beside, a), acc_up)
    acc_dn = lax.fori_loop(0, 1 - core, lambda _, a: add_source(1, beside, a), acc_dn)

    alternate = jnp.where(iota((8, 128), 0) % 2 == 0, np.float32(1), np.float32(-1))
    last = jnp.sum((flip * acc_dn[-1] - acc_up[-1]) * alternate, axis=0, keepdims=True)
    last = jnp.broadcast_to(last, (8, 128))
    last = swapped(last)
    last = jnp.where(((lane8 == 0) | (lane8 == 32)) & (gx == 0), last, 0.0) * np.float32(corner)

    row16 = iota((16, 128), 0)
    field = []
    for p in range(2):
        out = jnp.zeros((16, 128), F32)
        for w in range(WINDOWS):
            sums = acc_up[2 * w + p] + flip * acc_dn[2 * (WINDOWS - 1 - w) + p]
            if p == 1:
                sign = np.float32((1 if w % 2 else -1) / 8)
                sums = sums + sign * last
            line = jnp.sum(sums, axis=0, keepdims=True)
            out = jnp.where(row16 == w, jnp.broadcast_to(line, (16, 128)), out)
        field.append(out)

    turned = []
    for g in range(nx):
        c, s = twist[0, g : g + 1, :], twist[1, g : g + 1, :]
        turned.append(
            jnp.concatenate([field[0] * c - field[1] * s, field[0] * s + field[1] * c], axis=1)
        )
    shares = wide_dot(jnp.concatenate(turned, axis=0), q_high[...], q_low[...], (1, 0))
    send_c[...] = shares.reshape(nx, 16, 128)

    @pl.loop(1, nx)
    def _(o):
        to = lax.rem(gx + o, nx)
        remote(send_c.at[to], b_c.at[gx], s_c, r_c, (to, gy)).start()

    b_c[gx] = send_c[gx]
    atom = iota((128, 256), 1)
    want = jnp.where(atom < 128, atom >> 2, jnp.where(atom < 192, 97, 96))
    scale = jnp.where(atom < 128, 32, 2)
    hot = [
        jnp.where(iota((128, 256), 0) == want + scale * c, 1.0, 0.0).astype(BF16) for c in range(3)
    ]
    row8 = iota((8, 256), 0)

    blocks(b_c, nx - 1, s_c, r_c).wait_recv()
    whole = b_c[0]
    for g in range(1, nx):
        whole = whole + b_c[g]

    for c in range(3):
        dip[c, 0] = whole[1:9, 32 * c : 32 * c + 32]
        lines = exact_dot(whole, hot[c])

        def line(w):
            return jnp.broadcast_to(lines[w : w + 1], (8, 256))

        for t in range(4):
            dpl[c, pl.ds(8 * t, 8), :] = jnp.where(row8 < 4, line(2 * t + 1), line(2 * t + 2))
        dpl[c, pl.ds(32, 8), :] = jnp.where(row8 < 4, line(9), line(0))

    for sub in range(2):
        for z in range(4):
            v = [vec[sub, c, z] for c in range(3)]
            f = torque(v, [fix[sub, c, z] + dpl[c] for c in range(3)])
            p = normalized([a + np.float32(TIME_STEP) * b for a, b in zip(v, f)])
            coupling = cpl[sub, z]
            for c in range(3):
                wgt[sub, c, z] = coupling * p[c]
                fix[sub, c, z, 0:32, 0:128] = p[c][0:32, 0:128]
                nxt[sub, c, z] = f[c][0:32, 0:128]
    for sub in range(2):
        for z in range(4):
            cobalt = spc[sub, z] == 1
            ratio = pick(cobalt, ratio_pair)
            p = [fix[sub, c, z, 0:32, 0:128] for c in range(3)]
            h = [
                ratio * neighbours(sub, c, z)[0:32, 0:128] + dpl[c, 0:32, 0:128] for c in range(3)
            ]
            h[2] = h[2] + pick(cobalt, EASY_PAIR) * p[2]
            f = torque(p, h)
            w = [
                vec[sub, c, z, 0:32, 0:128] + np.float32(0.5 * TIME_STEP) * (nxt[sub, c, z] + f[c])
                for c in range(3)
            ]
            w = normalized(w)
            for c in range(3):
                nxt[sub, c, z] = w[c]

    for halo in halo_all:
        halo.wait_send()
    blocks(b_a, nx - 1, s_a, r_a).wait_send()
    blocks(b_c, nx - 1, s_c, r_c).wait_send()
    blocks(b_b.at[core], chips - 1, s_b, r_b).wait_send()
    hand_on.wait_send()


def solution(mesh):
    nx, ny = mesh.shape["gx"], mesh.shape["gy"]
    table, corner = wave_tables(nx, ny)
    base, phase, twist, lanes = trig_tables(nx)
    vmem = pl.BlockSpec(memory_space=pltpu.VMEM)
    anywhere = pl.BlockSpec(memory_space=pl.ANY)
    dma = pltpu.SemaphoreType.DMA
    regular = pltpu.SemaphoreType.REGULAR

    def scratch(*shape, dtype=F32):
        return pltpu.VMEM(shape, dtype)

    def on_device(spin_angles, species):
        return pl.pallas_call(
            functools.partial(step_kernel, nx, ny, corner),
            out_shape=[
                jax.ShapeDtypeStruct((2, 3, 4, 32, 128), F32),
                jax.ShapeDtypeStruct((3, 1, 8, 32), F32),
            ],
            in_specs=[anywhere] * 3 + [vmem] * 4,
            out_specs=[vmem] * 2,
            scratch_shapes=[
                scratch(2, 2, 4, 32, 128),
                scratch(2, 4, 32, 128, dtype=jnp.int32),
                scratch(3, 32, 128),
                scratch(8, 128),
                scratch(nx, 8, 128),
                scratch(256, 128, dtype=BF16),
                scratch(256, 128, dtype=BF16),
                scratch(2, TABLE_ROWS, 128),
                scratch(2, TABLE_ROWS, 128),
                scratch(2, 8, 128),
                scratch(2, 8, 128),
                scratch(2, ny // 2, 2, 8, 128),
                scratch(nx, 16, 128),
                scratch(nx, 16, 128),
                scratch(2, 8, 128),
                scratch(2, 2, 4, 2, 128),
                scratch(2, 4, 2, 128, dtype=jnp.int32),
                scratch(2, 8, 128),
                scratch(2, 2, 8, 128),
                scratch(6, 4, 40, 256),
                scratch(2, 4, 40, 256),
                scratch(2, 3, 4, 40, 256),
                scratch(2, 3, 4, 40, 256),
                scratch(2, 3, 4, 40, 256),
                scratch(3, 40, 256),
                dma((6,)),
                dma, dma, dma, dma, dma, dma, dma, dma,
                dma((4,)),
                dma((4,)),
                regular((ny // 8,)),
                regular((ny // 8,)),
            ],
            compiler_params=pltpu.CompilerParams(collective_id=0, has_side_effects=True),
        )(spin_angles, species, table, base, phase, twist, lanes)

    return jax.shard_map(
        lambda a, s: tuple(on_device(a, s)),
        mesh=mesh,
        in_specs=(P(None, None, None, "gy", "gx"), P(None, None, "gy", "gx")),
        out_specs=(P(None, None, None, "gy", "gx"), P(None, None, "gy", "gx")),
        check_vma=False,
    )
```

time: 60.7 us -> 53.3 us (0.88)
  Pallas kernels: 59.9 us -> 49.3 us
  local copies, waits for them, and re-layouts: 0 us -> 3.08 us
    pallas_call x2 -> x1, Pallas kernels: 59.9 us -> 49.3 us  [on_device(): pl.pallas_call(functools.partial(step_kernel, nx, ny, corner), out_shape=...]
    unnamed x0 -> x2, local copies, waits for them, and re-layouts: none -> 3.08 us
where the time goes in v2:
time: 53.3 us; the launch traced here: 53 us
  Pallas kernels  49.3 us (92%)
  local copies, waits for them, and re-layouts  3.08 us (6%)
  between operations  0.64 us (1%)
    pallas_call x1, Pallas kernels, on_device(): pl.pallas_call(functools.partial(step_kernel, nx, ny, corner), out_shape=...  49.3 us
    unnamed x2, local copies, waits for them, and re-layouts  3.08 us

profile of v2, /device:TPU:1, one launch (start us, length us, event | category | flops | bytes accessed | tf_op | source)
XLA Modules:
  0.0 53.0 jit_solution(10353252427983452281)
XLA Ops:
  0.6 49.3 %shard_map.86 = (f32[2,3,4,32,128]{4,3,2,1,0:T(8,128)}, f32[3,1,8,32]{3,2,1,0:T(8,128)}) custom-call(f32[2,2,4,32,128]{4,3,2,1,0:T(8,128)} %ang_hbm.1, s32[2,4,32,128]{3,2,1,0:T(8,128)} %spc_hbm.1, f32[17,400,128]{2,1,0:T(8,128)} %constant.10.clone.table_hbm, f32[2,32,128]{2,1,0:T(8,128)} %constant.11.clone.base, f32[16,2,128]{2,1,0:T(2,128)} %constant.12.clone.phase, ...), custom_call_target="tpu_custom_call" | custom-call | tf_op jit(solution)/shard_map/pallas_call | solution.py:590
  50.0 1.8 %copy.11 = f32[2,3,4,32,128]{4,3,2,1,0:T(8,128)} copy(f32[2,3,4,32,128]{4,3,2,1,0:T(8,128)} %get-tuple-element.4) | data formatting | bytes 786432
  51.7 1.3 %copy.12 = f32[3,1,8,32]{3,2,1,0:T(8,128)} copy(f32[3,1,8,32]{3,2,1,0:T(8,128)} %get-tuple-element.5) | data formatting | bytes 6144

commit v3 on v2

--- a/solution.py
+++ b/solution.py
@@ -26,6 +26,7 @@
 PART_K = 32
 ROWS = 8
 COLS = 32
+GROUPS = 4
 WINDOWS = 10
 TABLE_LEAD = 8
 TABLE_ROWS = 400
@@ -175,7 +176,7 @@
     nxt, dip,
     ang, spc, mom, tile, b_a, q_high, q_low, tab, tab2, up, dn, b_b, send_c, b_c, pack, g_ang, g_spc, g_x, g_c,
     raw, cpl, vec, wgt, fix, dpl,
-    load_sem, s_a, r_a, s_b, r_b, s_f, r_f, s_c, r_c, s_h, r_h, rise, fall,
+    load_sem, s_a, r_a, s_b, r_b, s_f, r_f, s_c, r_c, s_h, r_h, word,
 ):
     gx, gy = lax.axis_index("gx"), lax.axis_index("gy")
     left, right = lax.rem(gx + nx - 1, nx), lax.rem(gx + 1, nx)
@@ -184,11 +185,15 @@
     chip = gy // 2
     partner = gy + 1 - 2 * core
     chips = ny // 2
-    half = ny // 2
-    row = lax.rem(gy, half)
-    z_up = gy - row + lax.rem(row + 2, half)
-    z_down = gy - row + lax.rem(row + half - 2, half)
-    opposite = lax.rem(gy + half, ny)
+    nz = ny // 4
+    hops = nz // 2
+    side, z_own = chip // nz, lax.rem(chip, nz)
+
+    def at(across, dz):
+        there = (1 - side) if across else side
+        return 2 * (nz * there + lax.rem(z_own + dz + nz, nz)) + core
+
+    group = chips // GROUPS
 
     loads = []
     for sub in range(2):
@@ -210,13 +215,34 @@
     def _(o):
         signal(barrier, (lax.rem(gx + o, nx), gy))
 
-    for other in (above, below, z_up, z_down, opposite):
+    near = [above, below, at(True, 0), at(True, 1), at(True, -1)]
+    for dz in range(1, hops):
+        near += [at(False, dz), at(False, -dz)]
+    for other in near:
         signal(barrier, (gx, other))
 
     def remote(src, dst, send, recv, device):
         return pltpu.make_async_remote_copy(
             src_ref=src, dst_ref=dst, send_sem=send, recv_sem=recv, device_id=device, device_id_type=MESH
         )
+
+    b_cos, b_sin = base[0], base[1]
+    p_cos, p_sin = phase[gx, 0:1, :], phase[gx, 1:2, :]
+    cosine = b_cos * p_cos - b_sin * p_sin
+    sinus = b_sin * p_cos + b_cos * p_sin
+    comp, parity = lanes[0:1, :], lanes[1:2, :]
+    single = (iota((32, 128), 0) + gx) == 0
+
+    def store_q(at, q):
+        q_high[pl.ds(at, 32), :], q_low[pl.ds(at, 32), :] = split(q, 2)
+
+    for c in range(3):
+        mine = comp == np.float32(c)
+        real, imag = (sinus, cosine) if c == 1 else (cosine, -sinus)
+        store_q(32 * c, jnp.where(mine, jnp.where(single, 1.0, real), 0.0))
+        store_q(128 + 32 * c, jnp.where(mine, jnp.where(single, parity, imag), 0.0))
+    store_q(96, jnp.zeros((32, 128), F32))
+    store_q(224, jnp.zeros((32, 128), F32))
 
     total = [jnp.zeros((32, 128), F32) for _ in range(3)]
     for sub in range(2):
@@ -241,21 +267,16 @@
     packed = exact_dot(jnp.concatenate(rows, axis=1), spread)
     tile[...] = packed
 
-    pl.semaphore_wait(barrier, nx - 1 + 5)
+    pl.semaphore_wait(barrier, nx - 1 + len(near))
 
     @pl.loop(1, nx)
     def _(o):
         remote(tile, b_a.at[gx], s_a, r_a, (lax.rem(gx + o, nx), gy)).start()
 
-    def tell(t):
-        signal(rise.at[t], (gx, z_up))
-        signal(fall.at[t], (gx, z_down))
-
-    def hear(t):
-        pl.semaphore_wait(rise.at[t], 1)
-        pl.semaphore_wait(fall.at[t], 1)
-
-    hops = half // 4
+    signal(word.at[0], (gx, at(True, 0)))
+    signal(word.at[1], (gx, at(False, -1)))
+    signal(word.at[2], (gx, at(True, -1)))
+
     halo_row, halo_spc, halo_x, halo_c = [
         [remote(src, dst, s_h.at[n], r_h.at[n], to) for src, dst, to in pair]
         for n, pair in enumerate((
@@ -269,7 +290,6 @@
     ]
     halo_all = [remote(g, g, s_h.at[n], r_h.at[n], (gx, gy)) for n, g in enumerate((g_ang, g_spc, g_x, g_c))]
 
-    tell(0)
     b_a[gx] = packed
 
     lane = iota((128, 128), 1)
@@ -286,28 +306,55 @@
     pack[1] = edges[8:16]
     for copy in halo_x + halo_row + halo_spc:
         copy.start()
-    hear(0)
-    tell(1)
-
-    b_cos, b_sin = base[0], base[1]
-    p_cos, p_sin = phase[gx, 0:1, :], phase[gx, 1:2, :]
-    cosine = b_cos * p_cos - b_sin * p_sin
-    sinus = b_sin * p_cos + b_cos * p_sin
-    comp, parity = lanes[0:1, :], lanes[1:2, :]
-    single = (iota((32, 128), 0) + gx) == 0
-
-    def store_q(at, q):
-        q_high[pl.ds(at, 32), :], q_low[pl.ds(at, 32), :] = split(q, 2)
-
-    for c in range(3):
-        mine = comp == np.float32(c)
-        real, imag = (sinus, cosine) if c == 1 else (cosine, -sinus)
-        store_q(32 * c, jnp.where(mine, jnp.where(single, 1.0, real), 0.0))
-        store_q(128 + 32 * c, jnp.where(mine, jnp.where(single, parity, imag), 0.0))
-    store_q(96, jnp.zeros((32, 128), F32))
-    store_q(224, jnp.zeros((32, 128), F32))
-    hear(1)
-    tell(2)
+
+    def blocks(ref, n, send, recv):
+        return remote(ref.at[pl.ds(0, n)], ref.at[pl.ds(0, n)], send, recv, (gx, gy))
+
+    blocks(b_a, nx - 1, s_a, r_a).wait_recv()
+
+    wave = wide_dot(b_a[...].reshape(nx * 8, 128), q_high[...], q_low[...], (1, 1))
+    real = jnp.zeros((8, 128), F32)
+    imag = jnp.zeros((8, 128), F32)
+    for g in range(nx):
+        t_re, t_im = wave[8 * g : 8 * g + 8, 0:128], wave[8 * g : 8 * g + 8, 128:256]
+        c, s = twist[0, g : g + 1, :], twist[1, g : g + 1, :]
+        real = real + (t_re * c + t_im * s)
+        imag = imag + (t_im * c - t_re * s)
+
+    lane8 = iota((8, 128), 1)
+    is_y = (lane8 >= 32) & (lane8 < 64)
+    flip = jnp.where(is_y, np.float32(-1), np.float32(1))
+    dn[0] = real * flip
+    dn[1] = imag * flip
+    for r in range(8):
+        up[0, r : r + 1, :] = real[7 - r : 8 - r]
+        up[1, r : r + 1, :] = imag[7 - r : 8 - r]
+
+    for n in range(3):
+        pl.semaphore_wait(word.at[n], 1)
+
+    @pl.loop(0, chips - 1)
+    def _(k):
+        slot = chips - 1 - k
+        n, a = slot // 2, lax.rem(slot, 2)
+        odd = lax.rem(n, 2) == 1
+        steps = jnp.where(odd, (n + 1) // 2, nz - n // 2)
+        back = jnp.where((n == 0) | (n == nz - 1), n, jnp.where(odd, n + 1, n - 1))
+        there = 2 * back + a
+        to_chip = nz * jnp.where(a == 1, 1 - side, side) + lax.rem(z_own + steps, nz)
+        to = 2 * to_chip + core
+        land, mark = b_b.at[core, there], r_b.at[there // group]
+
+        @pl.when(to > gy)
+        def _():
+            remote(up, land, s_b, mark, (gx, to)).start()
+
+        @pl.when(to < gy)
+        def _():
+            remote(dn, land, s_b, mark, (gx, to)).start()
+
+    even = core == 0
+    b_b[core, 0] = jnp.where(even, up[...], dn[...])
 
     for load in late_loads:
         load.wait()
@@ -319,50 +366,6 @@
             pltpu.roll(t, 32, 1),
             jnp.where(wide < 64, -pltpu.roll(t, 64, 1), 0.0),
         )
-        hear(2 + p)
-        tell(3 + p)
-    for t in range(4, hops):
-        hear(t)
-        if t + 1 < hops:
-            tell(t + 1)
-
-    def blocks(ref, n, send, recv):
-        return remote(ref.at[pl.ds(0, n)], ref.at[pl.ds(0, n)], send, recv, (gx, gy))
-
-    blocks(b_a, nx - 1, s_a, r_a).wait_recv()
-
-    wave = wide_dot(b_a[...].reshape(nx * 8, 128), q_high[...], q_low[...], (1, 1))
-    real = jnp.zeros((8, 128), F32)
-    imag = jnp.zeros((8, 128), F32)
-    for g in range(nx):
-        t_re, t_im = wave[8 * g : 8 * g + 8, 0:128], wave[8 * g : 8 * g + 8, 128:256]
-        c, s = twist[0, g : g + 1, :], twist[1, g : g + 1, :]
-        real = real + (t_re * c + t_im * s)
-        imag = imag + (t_im * c - t_re * s)
-
-    lane8 = iota((8, 128), 1)
-    is_y = (lane8 >= 32) & (lane8 < 64)
-    flip = jnp.where(is_y, np.float32(-1), np.float32(1))
-    dn[0] = real * flip
-    dn[1] = imag * flip
-    for r in range(8):
-        up[0, r : r + 1, :] = real[7 - r : 8 - r]
-        up[1, r : r + 1, :] = imag[7 - r : 8 - r]
-
-    @pl.loop(1, chips)
-    def _(k):
-        to = lax.rem(gy + 2 * k, ny)
-
-        @pl.when(to > gy)
-        def _():
-            remote(up, b_b.at[core, chip], s_b, r_b, (gx, to)).start()
-
-        @pl.when(to < gy)
-        def _():
-            remote(dn, b_b.at[core, chip], s_b, r_b, (gx, to)).start()
-
-    even = core == 0
-    b_b[core, chip] = jnp.where(even, up[...], dn[...])
 
     halo_all[2].wait_recv()
     for copy in halo_c:
@@ -439,9 +442,13 @@
                     h = h + pick(cobalt, EASY_PAIR) * vec[sub, c, z]
                 fix[sub, c, z] = h
 
-    blocks(b_b.at[core], chips - 1, s_b, r_b).wait_recv()
-    hand_on = remote(b_b.at[core], b_b.at[core], s_f, r_f, (gx, partner))
-    hand_on.start()
+    def hand_on(g):
+        part = b_b.at[core, pl.ds(group * g, group)]
+        return remote(part, part, s_f.at[g], r_f.at[g], (gx, partner))
+
+    for g in range(GROUPS):
+        blocks(b_b.at[core], group - (g == 0), s_b, r_b.at[g]).wait_recv()
+        hand_on(g).start()
 
     zero = jnp.zeros((8, 128), F32)
 
@@ -461,7 +468,12 @@
 
     def add_chips(which, acc_up, acc_dn):
         def source(k):
-            return b_b[which, k, 0], b_b[which, k, 1]
+            ahead = lax.rem(lax.rem(k, nz) - z_own + nz, nz)
+            n = jnp.where(
+                ahead == 0, 0, jnp.where(ahead <= hops, 2 * ahead - 1, 2 * (nz - ahead))
+            )
+            slot = 2 * n + jnp.where(k // nz == side, 0, 1)
+            return b_b[which, slot, 0], b_b[which, slot, 1]
 
         acc_up = lax.fori_loop(
             0, chip, lambda k, a: add_source(gy - (2 * k + which), source(k), a), acc_up
@@ -474,9 +486,10 @@
     start = tuple(zero for _ in range(2 * WINDOWS + 1))
     acc_up = add_source(0, (up[0], up[1]), start)
     acc_up, acc_dn = add_chips(core, acc_up, start)
-    blocks(b_b.at[1 - core], chips, s_f, r_f).wait_recv()
+    for g in range(GROUPS):
+        hand_on(g).wait_recv()
     acc_up, acc_dn = add_chips(1 - core, acc_up, acc_dn)
-    beside = (b_b[1 - core, chip, 0], b_b[1 - core, chip, 1])
+    beside = (b_b[1 - core, 0, 0], b_b[1 - core, 0, 1])
     acc_up = lax.fori_loop(0, core, lambda _, a: add_source(1, beside, a), acc_up)
     acc_dn = lax.fori_loop(0, 1 - core, lambda _, a: add_source(1, beside, a), acc_dn)
 
@@ -511,7 +524,8 @@
     @pl.loop(1, nx)
     def _(o):
         to = lax.rem(gx + o, nx)
-        remote(send_c.at[to], b_c.at[gx], s_c, r_c, (to, gy)).start()
+        part = pl.ds(0, WINDOWS)
+        remote(send_c.at[to, part], b_c.at[gx, part], s_c, r_c, (to, gy)).start()
 
     b_c[gx] = send_c[gx]
     atom = iota((128, 256), 1)
@@ -522,7 +536,9 @@
     ]
     row8 = iota((8, 256), 0)
 
-    blocks(b_c, nx - 1, s_c, r_c).wait_recv()
+    all_c = b_c.at[pl.ds(0, nx - 1), pl.ds(0, WINDOWS)]
+    shares_in = remote(all_c, all_c, s_c, r_c, (gx, gy))
+    shares_in.wait_recv()
     whole = b_c[0]
     for g in range(1, nx):
         whole = whole + b_c[g]
@@ -569,9 +585,10 @@
     for halo in halo_all:
         halo.wait_send()
     blocks(b_a, nx - 1, s_a, r_a).wait_send()
-    blocks(b_c, nx - 1, s_c, r_c).wait_send()
-    blocks(b_b.at[core], chips - 1, s_b, r_b).wait_send()
-    hand_on.wait_send()
+    shares_in.wait_send()
+    blocks(b_b.at[core], chips - 1, s_b, r_b.at[0]).wait_send()
+    for g in range(GROUPS):
+        hand_on(g).wait_send()
 
 
 def solution(mesh):
@@ -622,11 +639,10 @@
                 scratch(2, 3, 4, 40, 256),
                 scratch(3, 40, 256),
                 dma((6,)),
-                dma, dma, dma, dma, dma, dma, dma, dma,
+                dma, dma, dma, dma((GROUPS,)), dma((GROUPS,)), dma((GROUPS,)), dma, dma,
                 dma((4,)),
                 dma((4,)),
-                regular((ny // 8,)),
-                regular((ny // 8,)),
+                regular((3,)),
             ],
             compiler_params=pltpu.CompilerParams(collective_id=0, has_side_effects=True),
         )(spin_angles, species, table, base, phase, twist, lanes)

time: 53.3 us -> 50.7 us (0.951)
  Pallas kernels: 49.3 us -> 46.7 us
    pallas_call x1, Pallas kernels: 49.3 us -> 46.7 us  [on_device(): pl.pallas_call(functools.partial(step_kernel, nx, ny, corner), out_shape=...]
where the time goes in v3:
time: 50.7 us; the launch traced here: 50.4 us
  Pallas kernels  46.7 us (92%)
  local copies, waits for them, and re-layouts  3.08 us (6%)
  between operations  0.64 us (1%)
    pallas_call x1, Pallas kernels, on_device(): pl.pallas_call(functools.partial(step_kernel, nx, ny, corner), out_shape=...  46.7 us
    unnamed x2, local copies, waits for them, and re-layouts  3.08 us

profile of v3, /device:TPU:1, one launch (start us, length us, event | category | flops | bytes accessed | tf_op | source)
XLA Modules:
  0.0 50.4 jit_solution(6198255462635307356)
XLA Ops:
  0.6 46.7 %shard_map.86 = (f32[2,3,4,32,128]{4,3,2,1,0:T(8,128)}, f32[3,1,8,32]{3,2,1,0:T(8,128)}) custom-call(f32[2,2,4,32,128]{4,3,2,1,0:T(8,128)} %ang_hbm.1, s32[2,4,32,128]{3,2,1,0:T(8,128)} %spc_hbm.1, f32[17,400,128]{2,1,0:T(8,128)} %constant.10.clone.table_hbm, f32[2,32,128]{2,1,0:T(8,128)} %constant.11.clone.base, f32[16,2,128]{2,1,0:T(2,128)} %constant.12.clone.phase, ...), custom_call_target="tpu_custom_call" | custom-call | tf_op jit(solution)/shard_map/pallas_call | solution.py:607
  47.3 1.8 %copy.11 = f32[2,3,4,32,128]{4,3,2,1,0:T(8,128)} copy(f32[2,3,4,32,128]{4,3,2,1,0:T(8,128)} %get-tuple-element.4) | data formatting | bytes 786432
  49.1 1.3 %copy.12 = f32[3,1,8,32]{3,2,1,0:T(8,128)} copy(f32[3,1,8,32]{3,2,1,0:T(8,128)} %get-tuple-element.5) | data formatting | bytes 6144

commit v4 on v3

--- a/solution.py
+++ b/solution.py
@@ -172,9 +172,9 @@
 
 def step_kernel(
     nx, ny, corner,
-    ang_hbm, spc_hbm, table_hbm, base, phase, twist, lanes,
-    nxt, dip,
-    ang, spc, mom, tile, b_a, q_high, q_low, tab, tab2, up, dn, b_b, send_c, b_c, pack, g_ang, g_spc, g_x, g_c,
+    ang_hbm, spc_hbm, table_hbm, base_hbm, phase_hbm, twist_hbm, lanes_hbm,
+    nxt, fld,
+    base, phase, twist, lanes, ang, spc, mom, tile, b_a, q_high, q_low, tab, tab2, up, dn, b_b, send_c, b_c, pack, g_ang, g_spc, g_x, g_c,
     raw, cpl, vec, wgt, fix, dpl,
     load_sem, s_a, r_a, s_b, r_b, s_f, r_f, s_c, r_c, s_h, r_h, word,
 ):
@@ -203,7 +203,13 @@
         pltpu.make_async_copy(table_hbm.at[gx], tab.at[0], load_sem.at[4]),
         pltpu.make_async_copy(table_hbm.at[jnp.where(gx == 0, nx, gx)], tab.at[1], load_sem.at[5]),
     ]
-    for load in loads + late_loads:
+    small_loads = [
+        pltpu.make_async_copy(src, dst, load_sem.at[6 + n])
+        for n, (src, dst) in enumerate(
+            ((base_hbm, base), (phase_hbm.at[gx], phase), (lanes_hbm, lanes), (twist_hbm, twist))
+        )
+    ]
+    for load in small_loads + loads + late_loads:
         load.start()
 
     barrier = pltpu.get_barrier_semaphore()
@@ -226,8 +232,10 @@
             src_ref=src, dst_ref=dst, send_sem=send, recv_sem=recv, device_id=device, device_id_type=MESH
         )
 
+    for load in small_loads:
+        load.wait()
     b_cos, b_sin = base[0], base[1]
-    p_cos, p_sin = phase[gx, 0:1, :], phase[gx, 1:2, :]
+    p_cos, p_sin = phase[0:1, :], phase[1:2, :]
     cosine = b_cos * p_cos - b_sin * p_sin
     sinus = b_sin * p_cos + b_cos * p_sin
     comp, parity = lanes[0:1, :], lanes[1:2, :]
@@ -543,8 +551,8 @@
     for g in range(1, nx):
         whole = whole + b_c[g]
 
+    fld[...] = whole
     for c in range(3):
-        dip[c, 0] = whole[1:9, 32 * c : 32 * c + 32]
         lines = exact_dot(whole, hot[c])
 
         def line(w):
@@ -578,7 +586,6 @@
                 vec[sub, c, z, 0:32, 0:128] + np.float32(0.5 * TIME_STEP) * (nxt[sub, c, z] + f[c])
                 for c in range(3)
             ]
-            w = normalized(w)
             for c in range(3):
                 nxt[sub, c, z] = w[c]
 
@@ -591,12 +598,22 @@
         hand_on(g).wait_send()
 
 
+def finish_kernel(raw, fld, nxt, dip):
+    for c in range(3):
+        dip[c, 0] = fld[1:9, 32 * c : 32 * c + 32]
+    for sub in range(2):
+        for z in range(4):
+            w = normalized([raw[sub, c, z] for c in range(3)])
+            for c in range(3):
+                nxt[sub, c, z] = w[c]
+
+
 def solution(mesh):
     nx, ny = mesh.shape["gx"], mesh.shape["gy"]
     table, corner = wave_tables(nx, ny)
     base, phase, twist, lanes = trig_tables(nx)
     vmem = pl.BlockSpec(memory_space=pltpu.VMEM)
-    anywhere = pl.BlockSpec(memory_space=pl.ANY)
+    hbm = pl.BlockSpec(memory_space=pl.ANY)
     dma = pltpu.SemaphoreType.DMA
     regular = pltpu.SemaphoreType.REGULAR
 
@@ -604,15 +621,19 @@
         return pltpu.VMEM(shape, dtype)
 
     def on_device(spin_angles, species):
-        return pl.pallas_call(
+        raw, fld = pl.pallas_call(
             functools.partial(step_kernel, nx, ny, corner),
             out_shape=[
                 jax.ShapeDtypeStruct((2, 3, 4, 32, 128), F32),
-                jax.ShapeDtypeStruct((3, 1, 8, 32), F32),
+                jax.ShapeDtypeStruct((16, 128), F32),
             ],
-            in_specs=[anywhere] * 3 + [vmem] * 4,
+            in_specs=[hbm] * 7,
             out_specs=[vmem] * 2,
             scratch_shapes=[
+                scratch(2, PART_K, 128),
+                scratch(2, 128),
+                scratch(2, nx, 128),
+                scratch(2, 128),
                 scratch(2, 2, 4, 32, 128),
                 scratch(2, 4, 32, 128, dtype=jnp.int32),
                 scratch(3, 32, 128),
@@ -638,7 +659,7 @@
                 scratch(2, 3, 4, 40, 256),
                 scratch(2, 3, 4, 40, 256),
                 scratch(3, 40, 256),
-                dma((6,)),
+                dma((10,)),
                 dma, dma, dma, dma((GROUPS,)), dma((GROUPS,)), dma((GROUPS,)), dma, dma,
                 dma((4,)),
                 dma((4,)),
@@ -646,6 +667,15 @@
             ],
             compiler_params=pltpu.CompilerParams(collective_id=0, has_side_effects=True),
         )(spin_angles, species, table, base, phase, twist, lanes)
+        return pl.pallas_call(
+            finish_kernel,
+            out_shape=[
+                jax.ShapeDtypeStruct((2, 3, 4, 32, 128), F32),
+                jax.ShapeDtypeStruct((3, 1, 8, 32), F32),
+            ],
+            in_specs=[vmem] * 2,
+            out_specs=[vmem] * 2,
+        )(raw, fld)
 
     return jax.shard_map(
         lambda a, s: tuple(on_device(a, s)),

time: 50.7 us -> 48.7 us (0.961)
  local copies, waits for them, and re-layouts: 3.08 us -> 0 us
  Pallas kernels: 46.7 us -> 47.9 us
    unnamed x2 -> x0, local copies, waits for them, and re-layouts: 3.08 us -> none
    pallas_call x0 -> x1, Pallas kernels: none -> 1.82 us  [on_device(): pl.pallas_call(finish_kernel, out_shape=[jax.ShapeDtypeStruct((2, 3, 4, 3...]
    pallas_call x1, Pallas kernels: 46.7 us -> 46.1 us  [on_device(): pl.pallas_call(functools.partial(step_kernel, nx, ny, corner), out_shape=...]
where the time goes in v4:
time: 48.7 us; the launch traced here: 48.5 us
  Pallas kernels  47.9 us (98%)
  between operations  0.64 us (1%)
    pallas_call x1, Pallas kernels, on_device(): pl.pallas_call(functools.partial(step_kernel, nx, ny, corner), out_shape=...  46.1 us
    pallas_call x1, Pallas kernels, on_device(): pl.pallas_call(finish_kernel, out_shape=[jax.ShapeDtypeStruct((2, 3, 4, 3...  1.82 us

profile of v4, /device:TPU:1, one launch (start us, length us, event | category | flops | bytes accessed | tf_op | source)
XLA Modules:
  0.0 48.5 jit_solution(18180193932708391971)
XLA Ops:
  0.6 46.1 %shard_map.86 = (f32[2,3,4,32,128]{4,3,2,1,0:T(8,128)}, f32[16,128]{1,0:T(8,128)}) custom-call(f32[2,2,4,32,128]{4,3,2,1,0:T(8,128)} %ang_hbm.1, s32[2,4,32,128]{3,2,1,0:T(8,128)} %spc_hbm.1, f32[17,400,128]{2,1,0:T(8,128)} %constant.10.clone.table_hbm, f32[2,32,128]{2,1,0:T(8,128)} %constant.11.clone.base_hbm, f32[16,2,128]{2,1,0:T(2,128)} %constant.12.clone.phase_hbm, ...), custom_call_target="tpu_custom_call" | custom-call | tf_op jit(solution)/shard_map/pallas_call | solution.py:624
  46.7 1.8 %shard_map.87 = (f32[2,3,4,32,128]{4,3,2,1,0:T(8,128)}, f32[3,1,8,32]{3,2,1,0:T(8,128)}) custom-call(f32[2,3,4,32,128]{4,3,2,1,0:T(8,128)} %get-tuple-element.4.raw, f32[16,128]{1,0:T(8,128)} %get-tuple-element.5.fld), custom_call_target="tpu_custom_call" | custom-call | tf_op jit(solution)/shard_map/pallas_call | solution.py:670

commit v5 on v4

--- a/solution.py
+++ b/solution.py
@@ -26,7 +26,7 @@
 PART_K = 32
 ROWS = 8
 COLS = 32
-GROUPS = 4
+GROUPS = 6
 WINDOWS = 10
 TABLE_LEAD = 8
 TABLE_ROWS = 400

time: 48.7 us -> 48.7 us (level)
  no operation moved by 1% of the time
where the time goes in v5:
time: 48.7 us; the launch traced here: 48.6 us
  Pallas kernels  47.9 us (98%)
  between operations  0.64 us (1%)
    pallas_call x1, Pallas kernels, on_device(): pl.pallas_call(functools.partial(step_kernel, nx, ny, corner), out_shape=...  46.1 us
    pallas_call x1, Pallas kernels, on_device(): pl.pallas_call(finish_kernel, out_shape=[jax.ShapeDtypeStruct((2, 3, 4, 3...  1.82 us

profile of v5, /device:TPU:1, one launch (start us, length us, event | category | flops | bytes accessed | tf_op | source)
XLA Modules:
  0.0 48.6 jit_solution(14491493642132924408)
XLA Ops:
  0.6 46.1 %shard_map.86 = (f32[2,3,4,32,128]{4,3,2,1,0:T(8,128)}, f32[16,128]{1,0:T(8,128)}) custom-call(f32[2,2,4,32,128]{4,3,2,1,0:T(8,128)} %ang_hbm.1, s32[2,4,32,128]{3,2,1,0:T(8,128)} %spc_hbm.1, f32[17,400,128]{2,1,0:T(8,128)} %constant.10.clone.table_hbm, f32[2,32,128]{2,1,0:T(8,128)} %constant.11.clone.base_hbm, f32[16,2,128]{2,1,0:T(2,128)} %constant.12.clone.phase_hbm, ...), custom_call_target="tpu_custom_call" | custom-call | tf_op jit(solution)/shard_map/pallas_call | solution.py:624
  46.7 1.8 %shard_map.87 = (f32[2,3,4,32,128]{4,3,2,1,0:T(8,128)}, f32[3,1,8,32]{3,2,1,0:T(8,128)}) custom-call(f32[2,3,4,32,128]{4,3,2,1,0:T(8,128)} %get-tuple-element.4.raw, f32[16,128]{1,0:T(8,128)} %get-tuple-element.5.fld), custom_call_target="tpu_custom_call" | custom-call | tf_op jit(solution)/shard_map/pallas_call | solution.py:670

commit v6 on v5

--- a/solution.py
+++ b/solution.py
@@ -252,6 +252,9 @@
     store_q(96, jnp.zeros((32, 128), F32))
     store_q(224, jnp.zeros((32, 128), F32))
 
+    def far_first(o):
+        return 1 + lax.rem(o + nx // 2 - 2, nx - 1)
+
     total = [jnp.zeros((32, 128), F32) for _ in range(3)]
     for sub in range(2):
         loads[2 * sub].wait()
@@ -279,7 +282,8 @@
 
     @pl.loop(1, nx)
     def _(o):
-        remote(tile, b_a.at[gx], s_a, r_a, (lax.rem(gx + o, nx), gy)).start()
+        to = lax.rem(gx + far_first(o), nx)
+        remote(tile, b_a.at[gx], s_a, r_a, (to, gy)).start()
 
     signal(word.at[0], (gx, at(True, 0)))
     signal(word.at[1], (gx, at(False, -1)))
@@ -531,7 +535,7 @@
 
     @pl.loop(1, nx)
     def _(o):
-        to = lax.rem(gx + o, nx)
+        to = lax.rem(gx + far_first(o), nx)
         part = pl.ds(0, WINDOWS)
         remote(send_c.at[to, part], b_c.at[gx, part], s_c, r_c, (to, gy)).start()
 

time: 48.7 us -> 49 us (level)
  no operation moved by 1% of the time
where the time goes in v6:
time: 49 us; the launch traced here: 48.8 us
  Pallas kernels  48.2 us (98%)
  between operations  0.64 us (1%)
    pallas_call x1, Pallas kernels, on_device(): pl.pallas_call(functools.partial(step_kernel, nx, ny, corner), out_shape=...  46.4 us
    pallas_call x1, Pallas kernels, on_device(): pl.pallas_call(finish_kernel, out_shape=[jax.ShapeDtypeStruct((2, 3, 4, 3...  1.82 us

profile of v6, /device:TPU:1, one launch (start us, length us, event | category | flops | bytes accessed | tf_op | source)
XLA Modules:
  0.0 48.8 jit_solution(9088914659163864652)
XLA Ops:
  0.6 46.4 %shard_map.86 = (f32[2,3,4,32,128]{4,3,2,1,0:T(8,128)}, f32[16,128]{1,0:T(8,128)}) custom-call(f32[2,2,4,32,128]{4,3,2,1,0:T(8,128)} %ang_hbm.1, s32[2,4,32,128]{3,2,1,0:T(8,128)} %spc_hbm.1, f32[17,400,128]{2,1,0:T(8,128)} %constant.10.clone.table_hbm, f32[2,32,128]{2,1,0:T(8,128)} %constant.11.clone.base_hbm, f32[16,2,128]{2,1,0:T(2,128)} %constant.12.clone.phase_hbm, ...), custom_call_target="tpu_custom_call" | custom-call | tf_op jit(solution)/shard_map/pallas_call | solution.py:628
  47.0 1.8 %shard_map.87 = (f32[2,3,4,32,128]{4,3,2,1,0:T(8,128)}, f32[3,1,8,32]{3,2,1,0:T(8,128)}) custom-call(f32[2,3,4,32,128]{4,3,2,1,0:T(8,128)} %get-tuple-element.4.raw, f32[16,128]{1,0:T(8,128)} %get-tuple-element.5.fld), custom_call_target="tpu_custom_call" | custom-call | tf_op jit(solution)/shard_map/pallas_call | solution.py:674
